TPU v7x, 32 devices: a whole 2x2x4 slice. The times are simulated.
32 devices in a mesh: replica: 16 (over z, x, core), tensor: 2 (over y).
Axes of the slice: x: 2, y: 2, z: 4, core: 2. Of those that a mesh axis runs over, the one named last changes fastest.
Arguments:
- w_gate: bfloat16 [16, 1024, 3072], P('replica', None, 'tensor'), may hold values from -6 to 6
- w_up: bfloat16 [16, 1024, 3072], P('replica', None, 'tensor'), may hold values from -6 to 6
- w_down: bfloat16 [16, 3072, 1024], P('replica', 'tensor'), may hold values from -6 to 6
- pool: bfloat16 [16, 512, 1024], P('replica', None, 'tensor'), may hold values from -6 to 6
- rows_index: int32 [16, 2, 2, 128], P('replica'), may hold values from 0 to 511
- partners: int32 [2, 16], replicated, may hold values from 0 to 15, as said below
Outputs:
- new_gate: bfloat16 [16, 1024, 3072], P('replica', None, 'tensor')
- new_up: bfloat16 [16, 1024, 3072], P('replica', None, 'tensor')
- new_down: bfloat16 [16, 3072, 1024], P('replica', 'tensor')
Inputs may be any that keep to these rules, and one draw needn't show every extreme that they name: Each row pairs the 16 replicas: partners[r, partners[r, i]] equals i and partners[r, i] differs from i.
All inputs are finite; a program needn't handle non-finite values.
Results may differ from a plain program's by a relative error of at most 0.029.
Values may be sent and summed in bfloat16 or wider, within the bound.
A program may use at most 128 MiB of HBM per device.

v0:
```python
import jax
import jax.numpy as jnp
from jax import lax
from jax.sharding import PartitionSpec as P

D = 1024
FF = 3072
ROUNDS = 2


inner_rate = 1.0
outer_rate = 0.5
momentum_rate = 0.9


def local_step(weights, pool_cols, picked):
    w_gate, w_up, w_down = weights
    in_scale = D ** (-0.5)
    hid_scale = FF ** (-0.5)
    in_cols = jnp.take(pool_cols, picked[0], axis=0)
    out_cols = jnp.take(pool_cols, picked[1], axis=0)
    inputs, targets = (
        lax.all_gather(in_cols, "tensor", axis=1, tiled=True),
        lax.all_gather(out_cols, "tensor", axis=1, tiled=True),
    )
    gate_pre = jnp.dot(inputs, w_gate, preferred_element_type=jnp.float32) * in_scale
    up_value = jnp.dot(inputs, w_up, preferred_element_type=jnp.float32) * in_scale
    sigmoid_gate = jax.nn.sigmoid(gate_pre)
    active = gate_pre * sigmoid_gate
    hidden = (active * up_value).astype(jnp.bfloat16)
    partial_sum = jnp.dot(hidden, w_down, preferred_element_type=jnp.float32) * hid_scale
    branch = lax.psum(partial_sum.astype(jnp.bfloat16), "tensor").astype(jnp.float32)
    errors = (inputs.astype(jnp.float32) + branch - targets.astype(jnp.float32)).astype(
        jnp.bfloat16
    )
    back_grad = (
        lax.dot_general(
            errors, w_down, (((1,), (1,)), ((), ())), preferred_element_type=jnp.float32
        )
        * hid_scale
    )
    delta_gate = (
        back_grad * up_value * sigmoid_gate * (1.0 + gate_pre * (1.0 - sigmoid_gate))
    ).astype(jnp.bfloat16)
    delta_up = (back_grad * active).astype(jnp.bfloat16)
    contract_rows = (((0,), (0,)), ((), ()))
    grad_gate = (
        lax.dot_general(inputs, delta_gate, contract_rows, preferred_element_type=jnp.float32)
        * in_scale
    )
    grad_up = (
        lax.dot_general(inputs, delta_up, contract_rows, preferred_element_type=jnp.float32)
        * in_scale
    )
    grad_down = (
        lax.dot_general(hidden, errors, contract_rows, preferred_element_type=jnp.float32)
        * hid_scale
    )
    gradients = (grad_gate, grad_up, grad_down)
    return tuple(
        (
            (weight.astype(jnp.float32) - inner_rate * gradient).astype(jnp.bfloat16)
            for weight, gradient in zip(weights, gradients)
        )
    )


def outer_update(weight, stepped, partner_step, partner_moment):
    pair_mean = 0.5 * (stepped.astype(jnp.float32) + partner_step.astype(jnp.float32))
    outer_grad = weight.astype(jnp.float32) - pair_mean
    moment_new = momentum_rate * 0.5 * partner_moment.astype(jnp.float32) + outer_grad
    updated = weight.astype(jnp.float32) - outer_rate * (momentum_rate * moment_new + outer_grad)
    return (updated.astype(jnp.bfloat16), moment_new.astype(jnp.bfloat16))


def make_share(stepped, moment):
    return (0.475 * stepped.astype(jnp.float32) - 0.2025 * moment.astype(jnp.float32)).astype(
        jnp.bfloat16
    )


def final_update(weight, stepped, moment, partner_share):
    updated = (
        0.05 * weight.astype(jnp.float32)
        + 0.475 * stepped.astype(jnp.float32)
        - 0.2025 * moment.astype(jnp.float32)
        + partner_share.astype(jnp.float32)
    )
    return updated.astype(jnp.bfloat16)


def partner_copy(payload, partner_row):
    replica_count = lax.axis_size("replica")
    stacked = jnp.stack([member.reshape(replica_count, -1) for member in payload])
    placed = jnp.take(
        lax.all_to_all(stacked, "replica", split_axis=1, concat_axis=1, tiled=True),
        partner_row,
        axis=1,
    )
    arrived = lax.all_to_all(placed, "replica", split_axis=1, concat_axis=1, tiled=True)
    return tuple(
        (arrived[index_mem].reshape(initial.shape) for index_mem, initial in enumerate(payload))
    )


def body(w_gate, w_up, w_down, pool, rows_index, partners):
    weights = (w_gate[0], w_up[0], w_down[0])
    moments = tuple((jnp.zeros_like(weight) for weight in weights))
    pool_cols = pool[0]
    for outer_step in range(ROUNDS):
        partner_row = partners[outer_step]
        picked = rows_index[0, outer_step]
        last_round = outer_step == ROUNDS - 1
        partner_share = None
        if last_round:
            stepped = local_step(weights, pool_cols, picked)
            own_share = tuple(
                (make_share(stepped[index_mat], moments[index_mat]) for index_mat in range(3))
            )
            partner_share = partner_copy(own_share, partner_row)
        else:
            stepped = local_step(weights, pool_cols, picked)
            partner_step = partner_copy(stepped, partner_row)
            partner_moment = moments
        if last_round:
            weights = tuple(
                (
                    final_update(
                        weights[index_mat],
                        stepped[index_mat],
                        moments[index_mat],
                        partner_share[index_mat],
                    )
                    for index_mat in range(3)
                )
            )
        else:
            results = [
                outer_update(
                    weights[index_mat],
                    stepped[index_mat],
                    partner_step[index_mat],
                    partner_moment[index_mat],
                )
                for index_mat in range(3)
            ]
            weights = tuple((result_pair[0] for result_pair in results))
            moments = tuple((result_pair[1] for result_pair in results))
    return (weights[0][None], weights[1][None], weights[2][None])


def solution(mesh):
    return jax.shard_map(
        body,
        mesh=mesh,
        in_specs=(
            P("replica", None, "tensor"),
            P("replica", None, "tensor"),
            P("replica", "tensor", None),
            P("replica", None, "tensor"),
            P("replica", None, None, None),
            P(),
        ),
        out_specs=(
            P("replica", None, "tensor"),
            P("replica", None, "tensor"),
            P("replica", "tensor", None),
        ),
        check_vma=False,
    )
```

profile of v0, /device:TPU:11, one launch (start us, length us, event | category | flops | bytes accessed | tf_op | source)
XLA Modules:
  0.0 1592.2 jit_solution(1116380565003575753)
XLA Ops:
  26.3 19.5 %all-reduce.3.cloned.1.call-done = bf16[128,1024]{1,0:T(8,128)(2,1)} async-done(((bf16[128,1024]{1,0:T(8,128)(2,1)}), bf16[128,1024]{1,0:T(8,128)(2,1)}) %all-reduce.3.cloned.1.call-update) | async-done | bytes 262160 | tf_op jit(solution)/shard_map/psum | solution.py:32
  56.6 10.8 stack_reshape.24
  67.4 10.8 stack_reshape.25
  82.8 11.2 stack_reshape.26
  94.0 24.4 %pad_maximum_fusion = bf16[3,16,98304]{2,0,1:T(4,128)(2,1)} fusion(bf16[1,16,98304]{2,0,1:T(2,128)(2,1)} %stack_reshape.26, bf16[1,16,98304]{2,0,1:T(2,128)(2,1)} %stack_reshape.25, bf16[1,16,98304]{2,0,1:T(2,128)(2,1)} %stack_reshape.24), kind=kLoop, calls=%fused_computation.6 | loop fusion | flops 28311552 | bytes 18874368 | tf_op jit(solution)/shard_map/stack | solution.py:94
  118.4 7.6 all-to-all-start
  126.0 272.0 %all-to-all-done = bf16[3,16,98304]{2,0,1:T(4,128)(2,1)} async-done(((bf16[3,16,98304]{2,0,1:T(4,128)(2,1)}), bf16[3,16,98304]{2,0,1:T(4,128)(2,1)}, u32[]{:S(2)}, u32[]{:S(2)}) %all-to-all-start) | async-done | bytes 9437216 | tf_op jit(solution)/shard_map/all_to_all | solution.py:96
  398.1 17.2 %gather_fusion.2 = bf16[16,3,98304]{2,1,0:T(4,128)(2,1)} fusion(bf16[3,16,98304]{2,0,1:T(4,128)(2,1)} %all-to-all-done, s32[1024]{0:T(1024)S(1)} %pad_clamp_fusion.3), kind=kCustom, calls=%fused_computation.1.clone | custom fusion | bytes 18874432 | tf_op jit(solution)/shard_map/jit(_take)/gather | solution.py:95
  415.3 11.7 select_bitcast_fusion.1
  433.7 5.5 all_gather.14
  439.2 264.8 %all-to-all-done.1 = bf16[3,16,98304]{2,0,1:T(4,128)(2,1)} async-done(((bf16[3,16,98304]{2,0,1:T(4,128)(2,1)}), bf16[3,16,98304]{2,0,1:T(4,128)(2,1)}, u32[]{:S(2)}, u32[]{:S(2)}) %all-to-all-start.1) | async-done | bytes 9437216 | tf_op jit(solution)/shard_map/all_to_all | solution.py:100
  703.9 61.7 %fusion.29 = (f32[16,98304]{1,0:T(8,128)}, f32[16,98304]{1,0:T(8,128)}, f32[16,98304]{1,0:T(8,128)}) fusion(bf16[3,16,98304]{2,0,1:T(4,128)(2,1)} %all-to-all-done.1), kind=kLoop, calls=%fused_computation.63 | loop fusion | flops 4718592 | bytes 28311552 | tf_op jit(solution)/shard_map/convert_element_type | solution.py:69
  770.7 6.8 fusion.18
  782.6 6.9 fusion.16
  794.5 5.9 fusion.20
  803.6 5.8 all_gather.15
  809.4 15.5 all-reduce.5.cloned.1.call-done
  828.3 9.5 subtract_convert_fusion.1
  845.6 10.8 stack_reshape.27
  856.4 10.8 stack_reshape.28
  867.3 9.2 subtract_convert_fusion
  876.4 11.2 stack_reshape.29
  887.7 24.4 %pad_maximum_fusion.1 = bf16[3,16,98304]{2,0,1:T(4,128)(2,1)} fusion(bf16[1,16,98304]{2,0,1:T(2,128)(2,1)} %stack_reshape.29, bf16[1,16,98304]{2,0,1:T(2,128)(2,1)} %stack_reshape.28, bf16[1,16,98304]{2,0,1:T(2,128)(2,1)} %stack_reshape.27), kind=kLoop, calls=%fused_computation.7 | loop fusion | flops 28311552 | bytes 18874368 | tf_op jit(solution)/shard_map/stack | solution.py:94
  912.0 6.9 all-to-all-start.2
  918.9 272.2 %all-to-all-done.2 = bf16[3,16,98304]{2,0,1:T(4,128)(2,1)} async-done(((bf16[3,16,98304]{2,0,1:T(4,128)(2,1)}), bf16[3,16,98304]{2,0,1:T(4,128)(2,1)}, u32[]{:S(2)}, u32[]{:S(2)}) %all-to-all-start.2) | async-done | bytes 9437216 | tf_op jit(solution)/shard_map/all_to_all | solution.py:96
  1191.1 17.1 %gather_fusion.5 = bf16[16,3,98304]{2,1,0:T(4,128)(2,1)} fusion(bf16[3,16,98304]{2,0,1:T(4,128)(2,1)} %all-to-all-done.2, s32[1024]{0:T(1024)S(1)} %pad_clamp_fusion), kind=kCustom, calls=%fused_computation.5.clone | custom fusion | bytes 18874432 | tf_op jit(solution)/shard_map/jit(_take)/gather | solution.py:95
  1208.3 8.5 select_bitcast_fusion
  1216.8 276.8 %all_to_all.20 = bf16[3,16,98304]{2,0,1:T(4,128)(2,1)S(1)} all-to-all(bf16[3,16,98304]{2,0,1:T(4,128)(2,1)S(1)} %select_bitcast_fusion), channel_id=1, replica_groups=mesh['replica'=16,'tensor'=2] {'replica'}, dimensions={1} | all-to-all | bytes 18874368 | tf_op jit(solution)/shard_map/all_to_all | solution.py:100
  1493.6 55.9 %fusion.24 = (f32[16,98304]{1,0:T(8,128)}, f32[16,98304]{1,0:T(8,128)}, f32[16,98304]{1,0:T(8,128)}) fusion(bf16[3,16,98304]{2,0,1:T(4,128)(2,1)S(1)} %all_to_all.20), kind=kLoop, calls=%fused_computation.53 | loop fusion | flops 4718592 | bytes 28311552 | tf_op jit(solution)/shard_map/convert_element_type | solution.py:87
  1559.6 5.3 reshape.40
  1564.9 8.1 fusion.33
  1574.6 10.2 fusion.34
  (80 shorter events, 82.3 us)
Async XLA Ops:
  7.2 1.1 copy-start
  7.2 38.6 %all-reduce.3.cloned.1.call-start = ((), (), s32[]{:S(2)}) async-start(), calls=%async_computation.4 | async-start | bytes 524288 | tf_op jit(solution)/shard_map/psum | solution.py:32
  9.1 10.4 copy-start.2
  45.8 7.9 copy-start.9
  67.4 10.9 copy-start.13
  118.4 7.6 copy-start.14
  118.4 279.7 %all-to-all-start = ((bf16[3,16,98304]{2,0,1:T(4,128)(2,1)}), bf16[3,16,98304]{2,0,1:T(4,128)(2,1)}, u32[]{:S(2)}, u32[]{:S(2)}) async-start(bf16[3,16,98304]{2,0,1:T(4,128)(2,1)} %pad_maximum_fusion), calls=%async_computation | async-start | bytes 25165824 | tf_op jit(solution)/shard_map/all_to_all | solution.py:96
  427.0 277.0 %all-to-all-start.1 = ((bf16[3,16,98304]{2,0,1:T(4,128)(2,1)}), bf16[3,16,98304]{2,0,1:T(4,128)(2,1)}, u32[]{:S(2)}, u32[]{:S(2)}) async-start(bf16[3,16,98304]{2,0,1:T(4,128)(2,1)} %select_bitcast_fusion.1), calls=%async_computation.1 | async-start | bytes 25165824 | tf_op jit(solution)/shard_map/all_to_all | solution.py:100
  431.8 393.1 %all-reduce.5.cloned.1.call-start = ((), (), s32[]{:S(2)}) async-start(), calls=%async_computation.5 | async-start | bytes 524288 | tf_op jit(solution)/shard_map/psum | solution.py:32
  794.5 5.9 copy-start.4
  794.5 6.5 copy-start.7
  800.4 1.8 copy-start.3
  824.9 12.9 slice-start
  828.2 9.6 slice-start.1
  828.3 9.9 copy-start.5
  828.3 11.3 copy-start.10
  828.3 12.2 copy-start.11
  856.4 10.9 copy-start.12
  912.0 279.1 %all-to-all-start.2 = ((bf16[3,16,98304]{2,0,1:T(4,128)(2,1)}), bf16[3,16,98304]{2,0,1:T(4,128)(2,1)}, u32[]{:S(2)}, u32[]{:S(2)}) async-start(bf16[3,16,98304]{2,0,1:T(4,128)(2,1)} %pad_maximum_fusion.1), calls=%async_computation.2 | async-start | bytes 25165824 | tf_op jit(solution)/shard_map/all_to_all | solution.py:96
  1559.6 13.4 slice-start.2
  1564.9 8.1 copy-start.6
  1564.9 8.1 copy-start.8
  1564.9 9.7 slice-start.3
  1574.6 10.3 copy-start.1
Sparse Core Ops, SparseCore 0:
  20.9 24.7 all-reduce.2
  803.6 21.2 all-reduce.4
where the time goes:
time: 1600 us; the launch traced here: 1590 us
  waiting for transfers between devices  844 us (53%)
  blocking collectives  298 us (19%)
  other arithmetic  226 us (14%)
  local copies, waits for them, and re-layouts  139 us (9%)
  matrix products  51.5 us (3%)
  starting transfers between devices  19.4 us (1%)
    all_to_all x2, waiting for transfers between devices, partner_copy(): lax.all_to_all(stacked, 'replica', split_axis=1, concat_axis=1, tiled=True)  544 us
    all_to_all x1, blocking collectives, partner_copy(): lax.all_to_all(placed, 'replica', split_axis=1, concat_axis=1, tiled=True)  277 us
    all_to_all x1, waiting for transfers between devices, partner_copy(): lax.all_to_all(placed, 'replica', split_axis=1, concat_axis=1, tiled=True)  265 us
    another operation x6, local copies, waits for them, and re-layouts, partner_copy(): jnp.stack([member.reshape(replica_count, -1) for member in payload])  65.7 us
    convert_element_type x1, other arithmetic, outer_update(): partner_step.astype(jnp.float32)  61.7 us
    convert_element_type x1, other arithmetic, final_update(): partner_share.astype(jnp.float32)  55.9 us
    another operation x2, other arithmetic, partner_copy(): jnp.stack([member.reshape(replica_count, -1) for member in payload])  48.7 us
    psum x2, waiting for transfers between devices, local_step(): lax.psum(partial_sum.astype(jnp.bfloat16), 'tensor').astype(jnp.float32)  35 us
  transfers between devices with their start and end apart: 5, of which 5 were waited for; matrix products, arithmetic and copies ran while one was open for 0% of the time, Pallas kernels for 0%

commit v1 on v0

v1 whole, which is shorter than its diff:
```python
import jax
import jax.numpy as jnp
from jax import lax
from jax.sharding import PartitionSpec as P

ROUNDS = 2
inner_rate = 1.0
outer_rate = 0.5
momentum_rate = 0.9
AXES = ("replica", "tensor")
F32 = jnp.float32
BF16 = jnp.bfloat16


def bdot(a, b, ca, cb):
    return lax.dot_general(a, b, (((ca,), (cb,)), ((0,), (0,))), preferred_element_type=F32)


def local_step(weights, inputs, own_in, own_out, in_scale, hid_scale):
    w_gate, w_up, w_down = weights
    replicas, rows, dim = inputs.shape
    gate_pre = bdot(inputs, w_gate, 2, 2) * in_scale
    up_value = bdot(inputs, w_up, 2, 2) * in_scale
    sigmoid_gate = jax.nn.sigmoid(gate_pre)
    active = gate_pre * sigmoid_gate
    hidden = (active * up_value).astype(BF16)
    terms = (bdot(hidden, w_down, 2, 1) * hid_scale).astype(BF16)
    branch = lax.psum_scatter(
        terms.reshape(replicas * rows, dim), AXES, scatter_dimension=0, tiled=True
    ).astype(F32)
    own_err = (own_in.astype(F32) + branch - own_out.astype(F32)).astype(BF16)
    errors = lax.all_gather(own_err, AXES, axis=0, tiled=True).reshape(replicas, rows, dim)
    back_grad = bdot(errors, w_down, 2, 2) * hid_scale
    delta_gate = (
        back_grad * up_value * sigmoid_gate * (1.0 + gate_pre * (1.0 - sigmoid_gate))
    ).astype(BF16)
    delta_up = (back_grad * active).astype(BF16)
    grads = (
        bdot(delta_gate, inputs, 1, 1) * in_scale,
        bdot(delta_up, inputs, 1, 1) * in_scale,
        bdot(hidden, errors, 1, 1) * hid_scale,
    )
    return tuple((w.astype(F32) - inner_rate * g).astype(BF16) for w, g in zip(weights, grads))


def first_update(weight, stepped, partner):
    other = jnp.take(stepped, partner, axis=0)
    pair_mean = 0.5 * (stepped.astype(F32) + other.astype(F32))
    outer_grad = weight.astype(F32) - pair_mean
    updated = weight.astype(F32) - outer_rate * (momentum_rate * outer_grad + outer_grad)
    return updated.astype(BF16), outer_grad.astype(BF16)


def last_update(weight, stepped, moment, partner):
    own = 0.475 * stepped.astype(F32) - 0.2025 * moment.astype(F32)
    other = jnp.take(own.astype(BF16), partner, axis=0).astype(F32)
    return (0.05 * weight.astype(F32) + own + other).astype(BF16)


def body(w_gate, w_up, w_down, pool, rows_index, partners):
    nrep, nten = lax.axis_size("replica"), lax.axis_size("tensor")
    dim, units_home = w_gate.shape[1:]
    units = units_home // nrep
    in_scale, hid_scale = dim ** (-0.5), (units_home * nten) ** (-0.5)
    rows = rows_index.shape[3]

    def spread(w):
        return lax.all_to_all(w.reshape(nrep, units, dim), "replica", 0, 0, tiled=True)

    weights = (spread(w_gate[0].T), spread(w_up[0].T), spread(w_down[0]))

    picked = rows_index[0]
    in_cols = jnp.take(pool[0], picked[:, 0], axis=0)
    out_cols = jnp.take(pool[0], picked[:, 1], axis=0)
    t = lax.axis_index("tensor")
    own_rows = rows // nten
    full = lax.all_gather(in_cols, AXES, axis=0, tiled=False)
    full = full.reshape(nrep, nten, ROUNDS, rows, dim // nten)
    full = full.transpose(2, 0, 3, 1, 4).reshape(ROUNDS, nrep, rows, dim)
    targets = lax.all_gather(out_cols, "tensor", axis=2, tiled=True)
    own_out = lax.dynamic_slice_in_dim(targets, t * own_rows, own_rows, 1)
    own_in = lax.dynamic_index_in_dim(full, lax.axis_index("replica"), 1, keepdims=False)
    own_in = lax.dynamic_slice_in_dim(own_in, t * own_rows, own_rows, 1)

    moments = None
    for r in range(ROUNDS):
        stepped = local_step(weights, full[r], own_in[r], own_out[r], in_scale, hid_scale)
        if r < ROUNDS - 1:
            both = [first_update(w, s, partners[r]) for w, s in zip(weights, stepped)]
            weights = tuple(b[0] for b in both)
            moments = tuple(b[1] for b in both)
        else:
            weights = tuple(
                last_update(w, s, m, partners[r]) for w, s, m in zip(weights, stepped, moments)
            )

    def home(w):
        return lax.all_to_all(w, "replica", 0, 0, tiled=True).reshape(units_home, dim)

    return (home(weights[0]).T[None], home(weights[1]).T[None], home(weights[2])[None])


def solution(mesh):
    return jax.shard_map(
        body,
        mesh=mesh,
        in_specs=(
            P("replica", None, "tensor"),
            P("replica", None, "tensor"),
            P("replica", "tensor", None),
            P("replica", None, "tensor"),
            P("replica", None, None, None),
            P(),
        ),
        out_specs=(
            P("replica", None, "tensor"),
            P("replica", None, "tensor"),
            P("replica", "tensor", None),
        ),
        check_vma=False,
    )
```

time: 1600 us -> 1060 us (0.66)
  waiting for transfers between devices: 844 us -> 566 us
  other arithmetic: 226 us -> 34.9 us
  blocking collectives: 298 us -> 236 us
  local copies, waits for them, and re-layouts: 139 us -> 107 us
  matrix products: 51.5 us -> 74.1 us
    all_to_all x3, waiting for transfers between devices: 809 us -> 203 us  [the longest x2 141 us: spread(): lax.all_to_all(w.reshape(nrep, units, dim), 'replica', 0, 0, tiled=True)]
    unnamed x2 -> x7, waiting for transfers between devices: 0.03 us -> 217 us
    all_gather x0 -> x3, waiting for transfers between devices: none -> 147 us  [the longest x2 147 us: local_step(): lax.all_gather(own_err, AXES, axis=0, tiled=True)]
    convert_element_type x5 -> x4, other arithmetic: 137 us -> 34 us  [the longest x1 17 us: last_update(): return (0.05 * weight.astype(F32) + own + other).astype(BF16)]
    another operation x6 -> x0, local copies, waits for them, and re-layouts: 65.7 us -> none  [partner_copy(): jnp.stack([member.reshape(replica_count, -1) for member in payload])]
    all_to_all x1 -> x3, blocking collectives: 277 us -> 223 us  [the longest x2 149 us: home(): lax.all_to_all(w, 'replica', 0, 0, tiled=True).reshape(units_home, dim)]
    another operation x2 -> x0, other arithmetic: 48.7 us -> none  [partner_copy(): jnp.stack([member.reshape(replica_count, -1) for member in payload])]
    psum x2 -> x0, waiting for transfers between devices: 35 us -> none  [local_step(): lax.psum(partial_sum.astype(jnp.bfloat16), 'tensor').astype(jnp.float32)]
  transfers between devices with their start and end apart: 5 -> 8, of which waited for: 5 -> 7; matrix products, arithmetic and copies ran while one was open for 0% -> 7% of each run, Pallas kernels for 0% -> 0%
where the time goes in v1:
time: 1060 us; the launch traced here: 1050 us
  waiting for transfers between devices  566 us (53%)
  blocking collectives  236 us (22%)
  local copies, waits for them, and re-layouts  107 us (10%)
  matrix products  74.1 us (7%)
  other arithmetic  34.9 us (3%)
  starting transfers between devices  17.1 us (2%)
  between operations  14.2 us (1%)
    unnamed x7, waiting for transfers between devices  217 us
    all_to_all x2, blocking collectives, home(): lax.all_to_all(w, 'replica', 0, 0, tiled=True).reshape(units_home, dim)  149 us
    all_gather x2, waiting for transfers between devices, local_step(): lax.all_gather(own_err, AXES, axis=0, tiled=True)  147 us
    all_to_all x2, waiting for transfers between devices, spread(): lax.all_to_all(w.reshape(nrep, units, dim), 'replica', 0, 0, tiled=True)  141 us
    all_to_all x1, blocking collectives, spread(): lax.all_to_all(w.reshape(nrep, units, dim), 'replica', 0, 0, tiled=True)  74.4 us
    dot_general x14, matrix products, bdot(): lax.dot_general(a, b, (((ca,), (cb,)), ((0,), (0,))), preferred_element_t...  74.1 us
    all_to_all x1, waiting for transfers between devices, home(): lax.all_to_all(w, 'replica', 0, 0, tiled=True).reshape(units_home, dim)  62.4 us
    slice x3, local copies, waits for them, and re-layouts, body(): full[r]  23.1 us
  transfers between devices with their start and end apart: 8, of which 7 were waited for; matrix products, arithmetic and copies ran while one was open for 7% of the time, Pallas kernels for 0%

profile of v1, /device:TPU:11, one launch (start us, length us, event | category | flops | bytes accessed | tf_op | source)
XLA Modules:
  0.0 1049.5 jit_solution(9939334877915968844)
XLA Ops:
  10.2 4.6 copy.31
  14.9 6.5 all-to-all-start
  21.4 4.7 copy.34
  26.1 100.0 %all-to-all-done = bf16[16,96,1024]{2,1,0:T(8,128)(2,1)} async-done(((bf16[16,96,1024]{2,1,0:T(8,128)(2,1)}), bf16[16,96,1024]{2,1,0:T(8,128)(2,1)}, u32[]{:S(2)}, u32[]{:S(2)}) %all-to-all-start) | async-done | bytes 3145760 | tf_op jit(solution)/shard_map/all_to_all | solution.py:68
  126.1 74.4 %all_to_all.30 = bf16[16,96,1024]{2,1,0:T(8,128)(2,1)} all-to-all(bf16[16,96,1024]{2,1,0:T(8,128)(2,1)} %bitcast.101), channel_id=1, replica_groups=mesh['replica'=16,'tensor'=2] {'replica'}, dimensions={0} | all-to-all | bytes 6291456 | tf_op jit(solution)/shard_map/all_to_all | solution.py:68
  200.5 5.1 all-to-all-start.2
  205.6 6.0 fusion.44
  211.6 8.5 copy.33
  220.1 7.7 squeeze.45
  227.8 4.8 convolution_multiply_fusion.5
  234.6 40.9 %all-to-all-done.2 = bf16[16,96,1024]{2,1,0:T(8,128)(2,1)} async-done(((bf16[16,96,1024]{2,1,0:T(8,128)(2,1)}), bf16[16,96,1024]{2,1,0:T(8,128)(2,1)}, u32[]{:S(2)}, u32[]{:S(2)}) %all-to-all-start.2) | async-done | bytes 3145760 | tf_op jit(solution)/shard_map/all_to_all | solution.py:68
  275.6 5.2 multiply_convert_fusion.1
  282.5 12.2 %all_gather.17 = bf16[2,128,1024]{1,2,0:T(8,128)(2,1)S(1)} all-gather(bf16[2,128,512]{1,2,0:T(8,128)(2,1)S(1)} %broadcast_select_fusion.3), channel_id=1, replica_groups=mesh['replica'=16,'tensor'=2] {'tensor'}, dimensions={2}, use_global_device_ids=true | all-gather | bytes 786432 | tf_op jit(solution)/shard_map/all_gather | solution.py:80
  294.6 12.1 %copy.32 = bf16[2,16,128,2,512]{2,4,3,1,0:T(8,128)(2,1)} copy(bf16[2,16,128,2,512]{4,2,0,3,1:T(8,128)(2,1)} %bitcast.91) | data formatting | bytes 16777216 | tf_op jit(solution)/shard_map/transpose | solution.py:79
  306.7 96.3 %reduce-scatter.7.cloned.1.call-done = bf16[64,1024]{1,0:T(8,128)(2,1)} async-done(((bf16[2048,1024]{1,0:T(8,128)(2,1)}), bf16[64,1024]{1,0:T(8,128)(2,1)}) %reduce-scatter.7.cloned.1.call-update) | async-done | bytes 131088
  406.3 8.6 copy.38
  414.8 8.0 squeeze.49
  422.8 66.1 %all-gather.5.cloned.1.call-done = bf16[2048,1024]{1,0:T(8,128)(2,1)} async-done(((bf16[64,1024]{1,0:T(8,128)(2,1)}), bf16[2048,1024]{1,0:T(8,128)(2,1)}) %all-gather.5.cloned.1.call-update) | async-done | bytes 4194320 | tf_op jit(solution)/shard_map/all_gather | solution.py:32
  488.9 4.8 convolution_multiply_fusion.3
  494.6 5.4 fusion.12
  504.4 5.7 fusion.15
  514.5 4.5 fusion.18
  521.7 13.8 %fusion.19 = (bf16[16,96,1024]{2,1,0:T(8,128)(2,1)S(1)}, bf16[16,96,1024]{2,1,0:T(8,128)(2,1)S(1)}, bf16[16,96,1024]{2,1,0:T(8,128)(2,1)S(1)}) fusion(bf16[16,96,1024]{2,1,0:T(8,128)(2,1)} %all-to-all-done.2, bf16[16,96,1024]{2,1,0:T(8,128)(2,1)} %copy-done.10, bf16[16,96,1024]{2,1,0:T(8,128)(2,1)} %gather_fusion.4, pred[16]{0:T(512)(128)(4,1)S(1)} %get-tuple-element.19, ...), kind=kLoop, calls=%fused_computation.47 | loop fusion | flops 56623104 | bytes 37748752 | tf_op jit(solution)/shard_map/convert_element_type | solution.py:51
  542.7 120.2 %reduce-scatter.9.cloned.1.call-done = bf16[64,1024]{1,0:T(8,128)(2,1)} async-done(((bf16[2048,1024]{1,0:T(8,128)(2,1)}), bf16[64,1024]{1,0:T(8,128)(2,1)}) %reduce-scatter.9.cloned.1.call-update) | async-done | bytes 131088
  668.5 80.4 %all-gather.7.cloned.1.call-done = bf16[2048,1024]{1,0:T(8,128)(2,1)} async-done(((bf16[64,1024]{1,0:T(8,128)(2,1)}), bf16[2048,1024]{1,0:T(8,128)(2,1)}) %all-gather.7.cloned.1.call-update) | async-done | bytes 4194320 | tf_op jit(solution)/shard_map/all_gather | solution.py:32
  760.0 24.9 %fusion.23 = (bf16[16,96,1024]{2,1,0:T(8,128)(2,1)}, bf16[16,96,1024]{2,1,0:T(8,128)(2,1)}, bf16[16,96,1024]{2,1,0:T(8,128)(2,1)}, bf16[16,96,1024]{2,1,0:T(8,12...) fusion(bf16[16,96,1024]{2,1,0:T(8,128)(2,1)} %gather_fusion.4, ...), kind=kOutput, calls=%fused_computation.54 | convolution fusion | flops 475004928 | bytes 64356368 | tf_op jit(solution)/shard_map/dot_general | solution.py:16
  797.9 17.0 %fusion.10 = (bf16[16,96,1024]{2,1,0:T(8,128)(2,1)}, bf16[16,96,1024]{2,1,0:T(8,128)(2,1)S(1)}, bf16[16,96,1024]{2,1,0:T(8,128)(2,1)S(1)}) fusion(bf16[16,96,1024]{2,1,0:T(8,128)(2,1)S(1)} %get-tuple-element.28, bf16[16,96,1024]{2,1,0:T(8,128)(2,1)} %get-tuple-element.6, bf16[16,96,1024]{2,1,0:T(8,128)(2,1)} %get-tuple-element.35, ...), kind=kLoop, calls=%fused_computation.38 | loop fusion | flops 56623104 | bytes 47185936 | tf_op jit(solution)/shard_map/convert_element_type | solution.py:57
  814.8 74.3 %all_to_all.31 = bf16[16,96,1024]{2,1,0:T(8,128)(2,1)S(1)} all-to-all(bf16[16,96,1024]{2,1,0:T(8,128)(2,1)S(1)} %get-tuple-element.23), channel_id=1, replica_groups=mesh['replica'=16,'tensor'=2] {'replica'}, dimensions={0} | all-to-all | bytes 6291456 | tf_op jit(solution)/shard_map/all_to_all | solution.py:98
  889.1 74.7 %all_to_all.32 = bf16[16,96,1024]{2,1,0:T(8,128)(2,1)} all-to-all(bf16[16,96,1024]{2,1,0:T(8,128)(2,1)S(1)} %get-tuple-element.22), channel_id=1, replica_groups=mesh['replica'=16,'tensor'=2] {'replica'}, dimensions={0} | all-to-all | bytes 6291456 | tf_op jit(solution)/shard_map/all_to_all | solution.py:98
  963.9 5.1 all-to-all-start.5
  971.9 4.7 copy.42
  976.6 62.4 %all-to-all-done.5 = bf16[16,96,1024]{2,1,0:T(8,128)(2,1)} async-done(((bf16[16,96,1024]{2,1,0:T(8,128)(2,1)}), bf16[16,96,1024]{2,1,0:T(8,128)(2,1)}, u32[]{:S(2)}, u32[]{:S(2)}) %all-to-all-start.5) | async-done | bytes 3145760 | tf_op jit(solution)/shard_map/all_to_all | solution.py:98
  (89 shorter events, 65.8 us)
Async XLA Ops:
  7.2 1.1 copy-start
  7.2 198.4 %all-gather.9.cloned.1.call-start = ((), (), s32[]{:S(2)}) async-start(), calls=%async_computation.10 | async-start | bytes 8650752 | tf_op jit(solution)/shard_map/all_gather | solution.py:77
  14.9 111.2 %all-to-all-start = ((bf16[16,96,1024]{2,1,0:T(8,128)(2,1)}), bf16[16,96,1024]{2,1,0:T(8,128)(2,1)}, u32[]{:S(2)}, u32[]{:S(2)}) async-start(bf16[16,96,1024]{2,1,0:T(8,128)(2,1)} %bitcast.100), calls=%async_computation | async-start | bytes 6291456 | tf_op jit(solution)/shard_map/all_to_all | solution.py:68
  200.5 75.1 %all-to-all-start.2 = ((bf16[16,96,1024]{2,1,0:T(8,128)(2,1)}), bf16[16,96,1024]{2,1,0:T(8,128)(2,1)}, u32[]{:S(2)}, u32[]{:S(2)}) async-start(bf16[16,96,1024]{2,1,0:T(8,128)(2,1)} %bitcast.106), calls=%async_computation.2 | async-start | bytes 6291456 | tf_op jit(solution)/shard_map/all_to_all | solution.py:68
  205.6 197.5 %reduce-scatter.7.cloned.1.call-start = ((), (), s32[]{:S(2)}) async-start(), calls=%async_computation.11 | async-start | bytes 4325376
  227.8 4.8 copy-start.2
  227.8 5.3 copy-start.6
  233.2 260.6 %copy-start.15 = (f32[16,128,96]{1,2,0:T(8,128)}, f32[16,128,96]{1,2,0:T(8,128)S(1)}, u32[]{:S(2)}) copy-start(f32[16,128,96]{1,2,0:T(8,128)S(1)} %convolution_multiply_fusion.5) | copy-start | bytes 2359300
  280.8 208.1 %all-gather.5.cloned.1.call-start = ((), (), s32[]{:S(2)}) async-start(), calls=%async_computation.8 | async-start | bytes 4325376 | tf_op jit(solution)/shard_map/all_gather | solution.py:32
  294.6 109.5 %copy-start.19 = (bf16[2,128,1024]{1,2,0:T(8,128)(2,1)}, bf16[2,128,1024]{1,2,0:T(8,128)(2,1)S(1)}, u32[]{:S(2)}) copy-start(bf16[2,128,1024]{1,2,0:T(8,128)(2,1)S(1)} %all_gather.17) | copy-start | bytes 1572868
  294.6 111.6 %copy-start.21 = (s32[2,16]{1,0:T(2,128)S(1)}, s32[2,16]{1,0:T(2,128)}, u32[]{:S(2)}) copy-start(s32[2,16]{1,0:T(2,128)} %param.15) | copy-start | bytes 388
  406.2 256.7 %reduce-scatter.9.cloned.1.call-start = ((), (), s32[]{:S(2)}) async-start(), calls=%async_computation.12 | async-start | bytes 4325376
  488.9 5.6 copy-start.3
  493.7 0.9 copy-start.18
  500.0 4.5 copy-start.7
  519.0 2.7 copy-start.10
  521.7 13.8 %copy-start.4 = (bf16[16,128,1024]{2,1,0:T(8,128)(2,1)S(1)}, bf16[16,128,1024]{2,1,0:T(8,128)(2,1)}, u32[]{:S(2)}) copy-start(bf16[16,128,1024]{2,1,0:T(8,128)(2,1)} %squeeze.49) | copy-start | bytes 12582916
  535.6 3.9 copy-start.11
  535.6 3.9 copy-start.13
  537.0 2.4 copy-start.16
  542.7 206.2 %all-gather.7.cloned.1.call-start = ((), (), s32[]{:S(2)}) async-start(), calls=%async_computation.9 | async-start | bytes 4325376 | tf_op jit(solution)/shard_map/all_gather | solution.py:32
  748.9 3.8 copy-start.5
  748.9 4.4 copy-start.14
  748.9 4.5 copy-start.17
  753.4 3.1 copy-start.12
  753.4 3.1 copy-start.20
  756.5 3.5 copy-start.8
  756.5 3.5 copy-start.9
  963.9 75.1 %all-to-all-start.5 = ((bf16[16,96,1024]{2,1,0:T(8,128)(2,1)}), bf16[16,96,1024]{2,1,0:T(8,128)(2,1)}, u32[]{:S(2)}, u32[]{:S(2)}) async-start(bf16[16,96,1024]{2,1,0:T(8,128)(2,1)} %get-tuple-element.21), calls=%async_computation.5 | async-start | bytes 6291456 | tf_op jit(solution)/shard_map/all_to_all | solution.py:98
  971.9 70.9 %copy-start.1 = (bf16[1,512,512]{2,1,0:T(8,128)(2,1)S(1)}, bf16[1,512,512]{2,1,0:T(8,128)(2,1)}, u32[]{:S(2)}) copy-start(bf16[1,512,512]{2,1,0:T(8,128)(2,1)} %param.13) | copy-start | bytes 1572868
Sparse Core Ops, SparseCore 0:
  11.7 120.6 all-gather.8
  280.9 122.1 reduce-scatter.6
  406.6 82.3 all-gather.4
  542.8 120.0 reduce-scatter.8
  668.6 80.2 all-gather.6

commit v2 on v1

--- a/solution.py
+++ b/solution.py
@@ -1,6 +1,10 @@
+import functools
+
 import jax
 import jax.numpy as jnp
 from jax import lax
+from jax.experimental import pallas as pl
+from jax.experimental.pallas import tpu as pltpu
 from jax.sharding import PartitionSpec as P
 
 ROUNDS = 2
@@ -16,7 +20,158 @@
     return lax.dot_general(a, b, (((ca,), (cb,)), ((0,), (0,))), preferred_element_type=F32)
 
 
-def local_step(weights, inputs, own_in, own_out, in_scale, hid_scale):
+def home_step(weights, inputs, targets, in_scale, hid_scale):
+    w_gate, w_up, w_down = weights
+    rows_last = (((1,), (1,)), ((), ()))
+    gate_pre = lax.dot_general(w_gate, inputs, rows_last, preferred_element_type=F32) * in_scale
+    up_value = lax.dot_general(w_up, inputs, rows_last, preferred_element_type=F32) * in_scale
+    sigmoid_gate = jax.nn.sigmoid(gate_pre)
+    active = gate_pre * sigmoid_gate
+    hidden = (active * up_value).astype(BF16)
+    term = lax.dot_general(
+        hidden, w_down, (((0,), (0,)), ((), ())), preferred_element_type=F32
+    ) * hid_scale
+    branch = lax.psum(term.astype(BF16), "tensor").astype(F32)
+    errors = (inputs.astype(F32) + branch - targets.astype(F32)).astype(BF16)
+    back = lax.dot_general(w_down, errors, rows_last, preferred_element_type=F32) * hid_scale
+    delta_gate = (
+        back * up_value * sigmoid_gate * (1.0 + gate_pre * (1.0 - sigmoid_gate))
+    ).astype(BF16)
+    delta_up = (back * active).astype(BF16)
+    return (delta_gate, delta_up, hidden), errors
+
+
+def flip(index, bit):
+    return index + bit * (1 - 2 * ((index // bit) % 2))
+
+
+def exchange_kernel(plans, nrep, nten, terms, own_in, own_out, out, *scratch):
+    nbits = len(plans[0][1])
+    nplan = len(plans)
+    tbits = nten.bit_length() - 1
+    bufs, (send_sem, recv_sem) = scratch[: -2], scratch[-2:]
+    rep, ten = lax.axis_index("replica"), lax.axis_index("tensor")
+
+    def bit_of(k):
+        return (ten // (1 << k)) % 2 if k < tbits else (rep // (1 << (k - tbits))) % 2
+
+    def peer(k):
+        if k < tbits:
+            return (rep, flip(ten, 1 << k))
+        return (flip(rep, 1 << (k - tbits)), ten)
+
+    barrier = pltpu.get_barrier_semaphore()
+    for k in range(nbits):
+        pl.semaphore_signal(
+            barrier, inc=1, device_id=peer(k), device_id_type=pl.DeviceIdType.MESH
+        )
+    pl.semaphore_wait(barrier, nbits)
+
+    state = []
+    for index, (cols, order) in enumerate(plans):
+        state.append(dict(cols=cols, order=order, left=list(range(nbits))[::-1], cur=terms, own=True))
+
+    def start_half(p, s):
+        st = state[p]
+        k = st["order"][s]
+        pos = st["left"].index(k)
+        keep, give = [slice(None)] * len(st["left"]), [slice(None)] * len(st["left"])
+        keep[pos], give[pos] = bit_of(k), 1 - bit_of(k)
+        tail = (slice(None), pl.ds(st["cols"][0], st["cols"][1])) if st["own"] else (slice(None), slice(None))
+        buf = bufs[p * nbits + s]
+        copy = pltpu.make_async_remote_copy(
+            src_ref=st["cur"].at[tuple(give) + tail],
+            dst_ref=buf,
+            send_sem=send_sem.at[p, s],
+            recv_sem=recv_sem.at[p, s],
+            device_id=peer(k),
+            device_id_type=pl.DeviceIdType.MESH,
+        )
+        copy.start()
+        st.update(copy=copy, pos=pos, tail=tail, buf=buf)
+
+    def end_half(p, s):
+        st = state[p]
+        st["copy"].wait()
+        rest = len(st["left"]) - 1
+        k = st["order"][s]
+        for flat in range(1 << rest):
+            bits = [(flat >> (rest - 1 - i)) & 1 for i in range(rest)]
+            src = bits[: st["pos"]] + [bit_of(k)] + bits[st["pos"] :]
+            mine = st["cur"][tuple(src) + st["tail"]].astype(F32)
+            dst = tuple(bits) + (slice(None), slice(None))
+            st["buf"][dst] = (mine + st["buf"][dst].astype(F32)).astype(BF16)
+        st["left"].remove(k)
+        st.update(cur=st["buf"], own=False)
+
+    for p in range(nplan):
+        start_half(p, 0)
+    for s in range(nbits):
+        for p in range(nplan):
+            end_half(p, s)
+            if s + 1 < nbits:
+                start_half(p, s + 1)
+
+    def held(p, s):
+        fixed = state[p]["order"][: s + 1]
+        lead = [bit_of(k) if k in fixed else slice(None) for k in range(nbits)[::-1]]
+        return tuple(lead) + (slice(None), pl.ds(state[p]["cols"][0], state[p]["cols"][1]))
+
+    def start_double(p, s):
+        k = state[p]["order"][s]
+        where = held(p, s)
+        copy = pltpu.make_async_remote_copy(
+            src_ref=out.at[where],
+            dst_ref=out.at[where],
+            send_sem=send_sem.at[p, nbits + s],
+            recv_sem=recv_sem.at[p, nbits + s],
+            device_id=peer(k),
+            device_id_type=pl.DeviceIdType.MESH,
+        )
+        copy.start()
+        state[p]["copy"] = copy
+
+    for p in range(nplan):
+        first, count = state[p]["cols"]
+        sl = (slice(None), pl.ds(first, count))
+        error = own_in[sl].astype(F32) + state[p]["buf"][...].astype(F32) - own_out[sl].astype(F32)
+        out[held(p, nbits - 1)] = error.astype(BF16)
+        start_double(p, nbits - 1)
+    for s in range(nbits)[::-1]:
+        for p in range(nplan):
+            state[p]["copy"].wait()
+            if s > 0:
+                start_double(p, s - 1)
+
+
+def exchange(terms, own_in, own_out, nrep, nten):
+    rows, dim = own_in.shape
+    nbits = (nrep * nten).bit_length() - 1
+    tbits = nten.bit_length() - 1
+    ring = list(range(tbits)) + list(range(tbits + 1, nbits))
+    half = dim // 2
+    orders = ([tbits] + ring, [tbits] + ring[tbits:] + ring[:tbits])
+    plans = [((i * half, half), orders[i]) for i in range(2)]
+    view = (2,) * nbits + (rows, dim)
+    scratch = [
+        pltpu.VMEM((2,) * (nbits - 1 - s) + (rows, half), BF16) for _ in plans for s in range(nbits)
+    ]
+    scratch += [pltpu.SemaphoreType.DMA((2, 2 * nbits))] * 2
+    vmem = pl.BlockSpec(memory_space=pltpu.VMEM)
+    out = pl.pallas_call(
+        functools.partial(exchange_kernel, plans, nrep, nten),
+        out_shape=jax.ShapeDtypeStruct(view, BF16),
+        in_specs=[vmem] * 3,
+        out_specs=vmem,
+        scratch_shapes=scratch,
+        compiler_params=pltpu.CompilerParams(
+            collective_id=0, has_side_effects=True, vmem_limit_bytes=62 << 20
+        ),
+    )(terms.reshape(view), own_in, own_out)
+    return out.reshape(nrep, nten * rows, dim)
+
+
+def slice_step(weights, inputs, own_in, own_out, in_scale, hid_scale):
     w_gate, w_up, w_down = weights
     replicas, rows, dim = inputs.shape
     gate_pre = bdot(inputs, w_gate, 2, 2) * in_scale
@@ -25,11 +180,16 @@
     active = gate_pre * sigmoid_gate
     hidden = (active * up_value).astype(BF16)
     terms = (bdot(hidden, w_down, 2, 1) * hid_scale).astype(BF16)
-    branch = lax.psum_scatter(
-        terms.reshape(replicas * rows, dim), AXES, scatter_dimension=0, tiled=True
-    ).astype(F32)
-    own_err = (own_in.astype(F32) + branch - own_out.astype(F32)).astype(BF16)
-    errors = lax.all_gather(own_err, AXES, axis=0, tiled=True).reshape(replicas, rows, dim)
+    nrep, nten = lax.axis_size("replica"), lax.axis_size("tensor")
+    total = nrep * nten
+    if total & (total - 1) == 0 and total * own_in.size <= 1 << 22:
+        errors = exchange(terms, own_in, own_out, nrep, nten)
+    else:
+        branch = lax.psum_scatter(
+            terms.reshape(replicas * rows, dim), AXES, scatter_dimension=0, tiled=True
+        ).astype(F32)
+        own_err = (own_in.astype(F32) + branch - own_out.astype(F32)).astype(BF16)
+        errors = lax.all_gather(own_err, AXES, axis=0, tiled=True).reshape(replicas, rows, dim)
     back_grad = bdot(errors, w_down, 2, 2) * hid_scale
     delta_gate = (
         back_grad * up_value * sigmoid_gate * (1.0 + gate_pre * (1.0 - sigmoid_gate))
@@ -67,32 +227,41 @@
     def spread(w):
         return lax.all_to_all(w.reshape(nrep, units, dim), "replica", 0, 0, tiled=True)
 
-    weights = (spread(w_gate[0].T), spread(w_up[0].T), spread(w_down[0]))
+    at_home = (w_gate[0].T, w_up[0].T, w_down[0])
+    weights = tuple(spread(w) for w in at_home)
 
     picked = rows_index[0]
     in_cols = jnp.take(pool[0], picked[:, 0], axis=0)
     out_cols = jnp.take(pool[0], picked[:, 1], axis=0)
-    t = lax.axis_index("tensor")
+    r, t = lax.axis_index("replica"), lax.axis_index("tensor")
     own_rows = rows // nten
-    full = lax.all_gather(in_cols, AXES, axis=0, tiled=False)
-    full = full.reshape(nrep, nten, ROUNDS, rows, dim // nten)
-    full = full.transpose(2, 0, 3, 1, 4).reshape(ROUNDS, nrep, rows, dim)
-    targets = lax.all_gather(out_cols, "tensor", axis=2, tiled=True)
-    own_out = lax.dynamic_slice_in_dim(targets, t * own_rows, own_rows, 1)
-    own_in = lax.dynamic_index_in_dim(full, lax.axis_index("replica"), 1, keepdims=False)
-    own_in = lax.dynamic_slice_in_dim(own_in, t * own_rows, own_rows, 1)
-
-    moments = None
-    for r in range(ROUNDS):
-        stepped = local_step(weights, full[r], own_in[r], own_out[r], in_scale, hid_scale)
-        if r < ROUNDS - 1:
-            both = [first_update(w, s, partners[r]) for w, s in zip(weights, stepped)]
-            weights = tuple(b[0] for b in both)
-            moments = tuple(b[1] for b in both)
-        else:
-            weights = tuple(
-                last_update(w, s, m, partners[r]) for w, s, m in zip(weights, stepped, moments)
-            )
+
+    def mine(x, axis):
+        return lax.dynamic_slice_in_dim(x, t * own_rows, own_rows, axis)
+
+    both = lax.all_gather(jnp.stack([in_cols, out_cols]), "tensor", axis=3, tiled=True)
+    inputs, targets = both[0], both[1]
+    factors, errors = home_step(at_home, inputs[0], targets[0], in_scale, hid_scale)
+    full = lax.all_gather(mine(inputs, 1), AXES, axis=0, tiled=False)
+    full = full.transpose(1, 0, 2, 3).reshape(ROUNDS, nrep, rows, dim)
+    all_errors = lax.all_gather(mine(errors, 0), AXES, axis=0, tiled=True).reshape(nrep, rows, dim)
+    stacked = jnp.stack([f.reshape(nrep, units, rows) for f in factors], axis=1)
+    factors = lax.all_to_all(stacked, "replica", 0, 0, tiled=True)
+
+    sides = (full[0], full[0], all_errors)
+    scales = (in_scale, in_scale, hid_scale)
+    moments = []
+    updated = []
+    for i in range(3):
+        grad = bdot(factors[:, i], sides[i], 2, 1) * scales[i]
+        stepped = (weights[i].astype(F32) - inner_rate * grad).astype(BF16)
+        pair = first_update(weights[i], stepped, partners[0])
+        updated.append(pair[0])
+        moments.append(pair[1])
+    stepped = slice_step(
+        tuple(updated), full[1], mine(inputs[1], 0), mine(targets[1], 0), in_scale, hid_scale
+    )
+    weights = tuple(last_update(w, s, m, partners[1]) for w, s, m in zip(updated, stepped, moments))
 
     def home(w):
         return lax.all_to_all(w, "replica", 0, 0, tiled=True).reshape(units_home, dim)

time: 1060 us -> 794 us (0.75)
  waiting for transfers between devices: 566 us -> 357 us
  blocking collectives: 236 us -> 151 us
  Pallas kernels: 0 us -> 72.4 us
  local copies, waits for them, and re-layouts: 107 us -> 64.8 us
    unnamed x7 -> x4, waiting for transfers between devices: 217 us -> 0.07 us
    all_gather x3, waiting for transfers between devices: 147 us -> 22.4 us  [the longest x1 22.4 us: body(): lax.all_gather(jnp.stack([in_cols, out_cols]), 'tensor', axis=3, tiled=True)]
    all_to_all x2 -> x3, waiting for transfers between devices: 141 us -> 220 us  [spread(): lax.all_to_all(w.reshape(nrep, units, dim), 'replica', 0, 0, tiled=True)]
    all_to_all x1 -> x0, blocking collectives: 74.4 us -> none  [spread(): lax.all_to_all(w.reshape(nrep, units, dim), 'replica', 0, 0, tiled=True)]
    pallas_call x0 -> x1, Pallas kernels: none -> 72.4 us  [exchange(): pl.pallas_call(functools.partial(exchange_kernel, plans, nrep, nten), out...]
    all_to_all x0 -> x1, waiting for transfers between devices: none -> 30.4 us  [body(): factors = lax.all_to_all(stacked, 'replica', 0, 0, tiled=True)]
    psum x0 -> x1, waiting for transfers between devices: none -> 23.1 us  [home_step(): branch = lax.psum(term.astype(BF16), 'tensor').astype(F32)]
    slice x4 -> x5, local copies, waits for them, and re-layouts: 23.8 us -> 6.19 us  [the longest x1 5.38 us: body(): full[1]]
  transfers between devices with their start and end apart: 8 -> 9, of which waited for: 7 -> 7; matrix products, arithmetic and copies ran while one was open for 7% -> 7% of each run, Pallas kernels for 0% -> 0%
where the time goes in v2:
time: 794 us; the launch traced here: 792 us
  waiting for transfers between devices  357 us (45%)
  blocking collectives  151 us (19%)
  matrix products  73.3 us (9%)
  Pallas kernels  72.4 us (9%)
  local copies, waits for them, and re-layouts  64.8 us (8%)
  other arithmetic  33.5 us (4%)
  starting transfers between devices  26.9 us (3%)
  between operations  14 us (2%)
    all_to_all x3, waiting for transfers between devices, spread(): lax.all_to_all(w.reshape(nrep, units, dim), 'replica', 0, 0, tiled=True)  220 us
    all_to_all x2, blocking collectives, home(): lax.all_to_all(w, 'replica', 0, 0, tiled=True).reshape(units_home, dim)  151 us
    pallas_call x1, Pallas kernels, exchange(): pl.pallas_call(functools.partial(exchange_kernel, plans, nrep, nten), out...  72.4 us
    dot_general x10, matrix products, bdot(): lax.dot_general(a, b, (((ca,), (cb,)), ((0,), (0,))), preferred_element_t...  61.5 us
    all_to_all x1, waiting for transfers between devices, home(): lax.all_to_all(w, 'replica', 0, 0, tiled=True).reshape(units_home, dim)  60.7 us
    all_to_all x1, waiting for transfers between devices, body(): factors = lax.all_to_all(stacked, 'replica', 0, 0, tiled=True)  30.4 us
    psum x1, waiting for transfers between devices, home_step(): branch = lax.psum(term.astype(BF16), 'tensor').astype(F32)  23.1 us
    all_gather x1, waiting for transfers between devices, body(): lax.all_gather(jnp.stack([in_cols, out_cols]), 'tensor', axis=3, tiled=True)  22.4 us
  transfers between devices with their start and end apart: 9, of which 7 were waited for; matrix products, arithmetic and copies ran while one was open for 7% of the time, Pallas kernels for 0%

profile of v2, /device:TPU:11, one launch (start us, length us, event | category | flops | bytes accessed | tf_op | source)
XLA Modules:
  0.0 792.4 jit_solution(2357431594186344444)
XLA Ops:
  11.7 22.4 %all-gather.4.cloned.1.call-done = bf16[2,2,128,1024]{3,2,1,0:T(8,128)(2,1)} async-done(((bf16[2,2,128,512]{3,2,1,0:T(8,128)(2,1)}), bf16[2,2,128,1024]{3,2,1,0:T(8,128)(2,1)}) %all-gather.4.cloned.1.call-update) | async-done | bytes 1048592 | tf_op jit(solution)/shard_map/all_gather | solution.py:242
  41.8 23.1 %all-reduce.2.cloned.1.call-done = bf16[128,1024]{1,0:T(8,128)(2,1)} async-done(((bf16[128,1024]{1,0:T(8,128)(2,1)}), bf16[128,1024]{1,0:T(8,128)(2,1)}) %all-reduce.2.cloned.1.call-update) | async-done | bytes 262160 | tf_op jit(solution)/shard_map/psum | solution.py:34
  73.6 6.9 all-to-all-start.1
  80.5 4.6 copy.23
  85.1 30.4 %all-to-all-done.1 = bf16[16,3,96,128]{3,2,1,0:T(8,128)(2,1)S(1)} async-done(((bf16[16,3,96,128]{3,2,1,0:T(8,128)(2,1)}), bf16[16,3,96,128]{3,2,1,0:T(8,128)(2,1)S(1)}, u32[]{:S(2)}, u32[]{:S(2)}) %all-to-all-start.1) | async-done | bytes 1179680 | tf_op jit(solution)/shard_map/all_to_all | solution.py:249
  115.6 5.0 all-to-all-start
  121.4 87.6 %all-to-all-done = bf16[16,96,1024]{2,1,0:T(8,128)(2,1)} async-done(((bf16[16,96,1024]{2,1,0:T(8,128)(2,1)}), bf16[16,96,1024]{2,1,0:T(8,128)(2,1)}, u32[]{:S(2)}, u32[]{:S(2)}) %all-to-all-start) | async-done | bytes 3145760 | tf_op jit(solution)/shard_map/all_to_all | solution.py:228
  209.0 5.1 all-to-all-start.3
  214.1 4.6 copy.29
  218.7 91.4 %all-to-all-done.3 = bf16[16,96,1024]{2,1,0:T(8,128)(2,1)} async-done(((bf16[16,96,1024]{2,1,0:T(8,128)(2,1)}), bf16[16,96,1024]{2,1,0:T(8,128)(2,1)}, u32[]{:S(2)}, u32[]{:S(2)}) %all-to-all-start.3) | async-done | bytes 3145760 | tf_op jit(solution)/shard_map/all_to_all | solution.py:228
  310.1 4.6 all-to-all-start.2
  316.1 6.2 fusion.18
  322.3 4.3 gather_fusion.4
  326.6 5.4 fusion.71
  334.0 5.1 fusion.12
  339.1 4.3 gather_fusion.2
  343.3 41.0 %all-to-all-done.2 = bf16[16,96,1024]{2,1,0:T(8,128)(2,1)} async-done(((bf16[16,96,1024]{2,1,0:T(8,128)(2,1)}), bf16[16,96,1024]{2,1,0:T(8,128)(2,1)}, u32[]{:S(2)}, u32[]{:S(2)}) %all-to-all-start.2) | async-done | bytes 3145760 | tf_op jit(solution)/shard_map/all_to_all | solution.py:228
  384.3 6.2 fusion.15
  390.5 4.3 gather_fusion.3
  394.8 13.5 %fusion.19 = (bf16[16,96,1024]{2,1,0:T(8,128)(2,1)S(1)}, bf16[16,96,1024]{2,1,0:T(8,128)(2,1)S(1)}, bf16[16,96,1024]{2,1,0:T(8,128)(2,1)S(1)}) fusion(bf16[16,96,1024]{2,1,0:T(8,128)(2,1)} %all-to-all-done.3, bf16[16,96,1024]{2,1,0:T(8,128)(2,1)} %fusion.18, bf16[16,96,1024]{2,1,0:T(8,128)(2,1)} %gather_fusion.4, pred[16]{0:T(512)(128)(4,1)S(1)} %get-tuple-element.23, ...), kind=kLoop, calls=%fused_computation.46 | loop fusion | flops 56623104 | bytes 37748752 | tf_op jit(solution)/shard_map/convert_element_type | solution.py:211
  415.4 72.4 %shard_map.85 = bf16[2,2,2,2,2,64,1024]{6,5,4,3,2,1,0:T(8,128)(2,1)} custom-call(bf16[2,2,2,2,2,64,1024]{6,5,4,3,2,1,0:T(8,128)(2,1)} %bitcast.141, bf16[64,1024]{1,0:T(8,128)(2,1)} %dynamic-slice_bitcast_fusion.1.own_in, bf16[64,1024]{1,0:T(8,128)(2,1)} %dynamic-slice_bitcast_fusion.own_out), custom_call_target="tpu_custom_call" | custom-call | tf_op jit(solution)/shard_map/pallas_call | solution.py:161
  487.9 4.8 convolution_multiply_fusion
  499.8 25.6 %fusion.23 = (bf16[16,96,1024]{2,1,0:T(8,128)(2,1)}, bf16[16,96,1024]{2,1,0:T(8,128)(2,1)}, bf16[16,96,1024]{2,1,0:T(8,128)(2,1)}, bf16[16,96,1024]{2,1,0:T(8,12...) fusion(bf16[16,96,1024]{2,1,0:T(8,128)(2,1)} %gather_fusion.4, ...), kind=kOutput, calls=%fused_computation.53 | convolution fusion | flops 475004928 | bytes 64356368 | tf_op jit(solution)/shard_map/dot_general | solution.py:20
  525.4 4.3 gather_fusion.5
  533.9 4.3 gather_fusion.7
  538.2 17.7 %fusion.10 = (bf16[16,96,1024]{2,1,0:T(8,128)(2,1)}, bf16[16,96,1024]{2,1,0:T(8,128)(2,1)S(1)}, bf16[16,96,1024]{2,1,0:T(8,128)(2,1)S(1)}) fusion(bf16[16,96,1024]{2,1,0:T(8,128)(2,1)} %copy-done.2, bf16[16,96,1024]{2,1,0:T(8,128)(2,1)} %get-tuple-element.6, bf16[16,96,1024]{2,1,0:T(8,128)(2,1)} %get-tuple-element.39, ...), kind=kLoop, calls=%fused_computation.37 | loop fusion | flops 56623104 | bytes 47185936 | tf_op jit(solution)/shard_map/convert_element_type | solution.py:217
  555.9 76.3 %all_to_all.35 = bf16[16,96,1024]{2,1,0:T(8,128)(2,1)} all-to-all(bf16[16,96,1024]{2,1,0:T(8,128)(2,1)S(1)} %get-tuple-element.27), channel_id=1, replica_groups=mesh['replica'=16,'tensor'=2] {'replica'}, dimensions={0} | all-to-all | bytes 6291456 | tf_op jit(solution)/shard_map/all_to_all | solution.py:267
  632.2 74.7 %all_to_all.36 = bf16[16,96,1024]{2,1,0:T(8,128)(2,1)} all-to-all(bf16[16,96,1024]{2,1,0:T(8,128)(2,1)S(1)} %get-tuple-element.26), channel_id=1, replica_groups=mesh['replica'=16,'tensor'=2] {'replica'}, dimensions={0} | all-to-all | bytes 6291456 | tf_op jit(solution)/shard_map/all_to_all | solution.py:267
  707.0 5.1 all-to-all-start.6
  712.1 4.6 copy.32
  716.7 4.7 copy.33
  721.4 60.7 %all-to-all-done.6 = bf16[16,96,1024]{2,1,0:T(8,128)(2,1)} async-done(((bf16[16,96,1024]{2,1,0:T(8,128)(2,1)}), bf16[16,96,1024]{2,1,0:T(8,128)(2,1)}, u32[]{:S(2)}, u32[]{:S(2)}) %all-to-all-start.6) | async-done | bytes 3145760 | tf_op jit(solution)/shard_map/all_to_all | solution.py:267
  (79 shorter events, 47.4 us)
Async XLA Ops:
  7.2 1.1 copy-start
  7.2 26.9 %all-gather.4.cloned.1.call-start = ((), (), s32[]{:S(2)}) async-start(), calls=%async_computation.7 | async-start | bytes 1572864 | tf_op jit(solution)/shard_map/all_gather | solution.py:242
  11.6 53.2 %all-reduce.2.cloned.1.call-start = ((), (), s32[]{:S(2)}) async-start(), calls=%async_computation.8 | async-start | bytes 524288 | tf_op jit(solution)/shard_map/psum | solution.py:34
  36.6 3.7 copy-start.12
  36.6 28.2 %copy-start.13 = (bf16[2,2,128,1024]{3,2,1,0:T(8,128)(2,1)S(1)}, bf16[2,2,128,1024]{3,2,1,0:T(8,128)(2,1)}, u32[]{:S(2)}) copy-start(bf16[2,2,128,1024]{3,2,1,0:T(8,128)(2,1)} %all-gather.4.cloned.1.call-done) | copy-start | bytes 3145732
  41.7 274.4 %all-gather.8.cloned.1.call-start = ((), (), s32[]{:S(2)}) async-start(), calls=%async_computation.10 | async-start | bytes 4325376 | tf_op jit(solution)/shard_map/all_gather | solution.py:247
  73.6 41.9 %all-to-all-start.1 = ((bf16[16,3,96,128]{3,2,1,0:T(8,128)(2,1)}), bf16[16,3,96,128]{3,2,1,0:T(8,128)(2,1)S(1)}, u32[]{:S(2)}, u32[]{:S(2)}) async-start(bf16[16,3,96,128]{3,2,1,0:T(8,128)(2,1)} %copy.27), calls=%async_computation.1 | async-start | bytes 2359296 | tf_op jit(solution)/shard_map/all_to_all | solution.py:249
  85.1 35.5 %slice-start = ((bf16[2,2,128,1024]{3,2,1,0:T(8,128)(2,1)}), bf16[1,2,128,1024]{3,2,1,0:T(8,128)(2,1)S(1)}, s32[]{:S(2)}) async-start(bf16[2,2,128,1024]{3,2,1,0:T(8,128)(2,1)} %all-gather.4.cloned.1.call-done), calls=%async_computation.11 | async-start | bytes 1048576 | tf_op jit(solution)/shard_map/slice | solution.py:243
  115.6 93.4 %all-to-all-start = ((bf16[16,96,1024]{2,1,0:T(8,128)(2,1)}), bf16[16,96,1024]{2,1,0:T(8,128)(2,1)}, u32[]{:S(2)}, u32[]{:S(2)}) async-start(bf16[16,96,1024]{2,1,0:T(8,128)(2,1)} %bitcast.144), calls=%async_computation | async-start | bytes 6291456 | tf_op jit(solution)/shard_map/all_to_all | solution.py:228
  120.6 206.0 %all-gather.6.cloned.1.call-start = ((), (), s32[]{:S(2)}) async-start(), calls=%async_computation.9 | async-start | bytes 8650752 | tf_op jit(solution)/shard_map/all_gather | solution.py:245
  209.0 101.2 %all-to-all-start.3 = ((bf16[16,96,1024]{2,1,0:T(8,128)(2,1)}), bf16[16,96,1024]{2,1,0:T(8,128)(2,1)}, u32[]{:S(2)}, u32[]{:S(2)}) async-start(bf16[16,96,1024]{2,1,0:T(8,128)(2,1)} %bitcast.147), calls=%async_computation.3 | async-start | bytes 6291456 | tf_op jit(solution)/shard_map/all_to_all | solution.py:228
  218.7 96.0 %copy-start.15 = (s32[2,16]{1,0:T(2,128)S(1)}, s32[2,16]{1,0:T(2,128)}, u32[]{:S(2)}) copy-start(s32[2,16]{1,0:T(2,128)} %param.15) | copy-start | bytes 388
  310.1 74.2 %all-to-all-start.2 = ((bf16[16,96,1024]{2,1,0:T(8,128)(2,1)}), bf16[16,96,1024]{2,1,0:T(8,128)(2,1)}, u32[]{:S(2)}, u32[]{:S(2)}) async-start(bf16[16,96,1024]{2,1,0:T(8,128)(2,1)} %bitcast.143), calls=%async_computation.2 | async-start | bytes 6291456 | tf_op jit(solution)/shard_map/all_to_all | solution.py:228
  332.0 2.0 copy-start.9
  394.8 13.6 %copy-start.4 = (bf16[1,32,64,1024]{3,2,0,1:T(8,128)(2,1)S(1)}, bf16[1,32,64,1024]{3,2,0,1:T(8,128)(2,1)}, u32[]{:S(2)}) copy-start(bf16[1,32,64,1024]{3,2,0,1:T(8,128)(2,1)} %get-tuple-element.15) | copy-start | bytes 12582916
  408.3 3.9 copy-start.7
  408.3 3.9 copy-start.10
  408.3 3.8 copy-start.2
  487.8 4.8 copy-start.5
  487.9 5.3 copy-start.11
  493.2 3.2 copy-start.8
  493.2 3.2 copy-start.14
  496.4 3.4 copy-start.3
  496.4 3.4 copy-start.6
  707.0 75.1 %all-to-all-start.6 = ((bf16[16,96,1024]{2,1,0:T(8,128)(2,1)}), bf16[16,96,1024]{2,1,0:T(8,128)(2,1)}, u32[]{:S(2)}, u32[]{:S(2)}) async-start(bf16[16,96,1024]{2,1,0:T(8,128)(2,1)} %get-tuple-element.25), calls=%async_computation.6 | async-start | bytes 6291456 | tf_op jit(solution)/shard_map/all_to_all | solution.py:267
  716.7 69.2 %copy-start.1 = (bf16[1,512,512]{2,1,0:T(8,128)(2,1)S(1)}, bf16[1,512,512]{2,1,0:T(8,128)(2,1)}, u32[]{:S(2)}) copy-start(bf16[1,512,512]{2,1,0:T(8,128)(2,1)} %param.13) | copy-start | bytes 1572868
Sparse Core Ops, SparseCore 0:
  11.8 22.2 all-gather.3
  41.8 22.9 all-reduce.1
  67.7 87.3 all-gather.7
  158.0 136.1 all-gather.5

commit v3 on v2

--- a/solution.py
+++ b/solution.py
@@ -171,6 +171,118 @@
     return out.reshape(nrep, nten * rows, dim)
 
 
+def dot_in(a, b):
+    return lax.dot_general(a, b, (((1,), (1,)), ((), ())), preferred_element_type=F32)
+
+
+def update_kernel(scales, partner, *refs):
+    own, other = refs[:6], refs[6:12]
+    x2 = refs[12]
+    new_w, new_m = refs[13:16], refs[16:19]
+    pre, hid, terms = refs[19:22]
+    in_scale, hid_scale = scales
+
+    def stepped(group, i, scale):
+        weight, fac, side = group[i][0], group[3][0, i], group[5 if i == 2 else 4][0]
+        grad = jnp.dot(fac, side, preferred_element_type=F32) * scale
+        return (weight.astype(F32) - inner_rate * grad).astype(BF16).astype(F32)
+
+    for i in range(3):
+        scale = hid_scale if i == 2 else in_scale
+        pair_mean = 0.5 * (stepped(own, i, scale) + stepped(other, i, scale))
+        weight = own[i][0].astype(F32)
+        outer_grad = weight - pair_mean
+        updated = weight - outer_rate * (momentum_rate * outer_grad + outer_grad)
+        new_w[i][0] = updated.astype(BF16)
+        new_m[i][0] = outer_grad.astype(BF16)
+    gate_pre = dot_in(new_w[0][0], x2[0]) * in_scale
+    up_value = dot_in(new_w[1][0], x2[0]) * in_scale
+    hidden = (gate_pre * jax.nn.sigmoid(gate_pre) * up_value).astype(BF16)
+    term = lax.dot_general(
+        hidden, new_w[2][0], (((0,), (0,)), ((), ())), preferred_element_type=F32
+    ) * hid_scale
+    pre[0, 0] = gate_pre
+    pre[0, 1] = up_value
+    hid[0] = hidden
+    terms[0] = term.astype(BF16)
+
+
+def last_kernel(scales, partner, *refs):
+    own, other, outs = refs[:10], refs[10:20], refs[20:]
+    in_scale, hid_scale = scales
+
+    def shares(group):
+        x2, e2, pre, hid = group[6][0], group[7][0], group[8], group[9][0]
+        gate_pre, up_value = pre[0, 0], pre[0, 1]
+        back = dot_in(group[2][0], e2) * hid_scale
+        sig = jax.nn.sigmoid(gate_pre)
+        delta_gate = (back * up_value * sig * (1.0 + gate_pre * (1.0 - sig))).astype(BF16)
+        delta_up = (back * (gate_pre * sig)).astype(BF16)
+        for i, (fac, side, scale) in enumerate(
+            ((delta_gate, x2, in_scale), (delta_up, x2, in_scale), (hid, e2, hid_scale))
+        ):
+            grad = jnp.dot(fac, side, preferred_element_type=F32) * scale
+            local = (group[i][0].astype(F32) - inner_rate * grad).astype(BF16).astype(F32)
+            yield 0.475 * local - 0.2025 * group[3 + i][0].astype(F32)
+
+    for i, (mine, theirs) in enumerate(zip(shares(own), shares(other))):
+        total = 0.05 * own[i][0].astype(F32) + mine + theirs.astype(BF16).astype(F32)
+        outs[i][0] = total.astype(BF16)
+
+
+def over_replicas(kernel, scales, partner, paired, single, out_shapes, flops):
+    nrep = partner.shape[0]
+
+    def spec(shape, swap):
+        zeros = (0,) * (len(shape) - 1)
+        if swap:
+            return pl.BlockSpec((1,) + shape[1:], lambda p, who: (who[p],) + zeros)
+        return pl.BlockSpec((1,) + shape[1:], lambda p, who: (p,) + zeros)
+
+    args = list(paired) + list(paired) + list(single)
+    swaps = [False] * len(paired) + [True] * len(paired) + [False] * len(single)
+    moved = sum(a.size * a.dtype.itemsize for a in args)
+    return pl.pallas_call(
+        functools.partial(kernel, scales),
+        grid_spec=pltpu.PrefetchScalarGridSpec(
+            num_scalar_prefetch=1,
+            grid=(nrep,),
+            in_specs=[spec(a.shape, w) for a, w in zip(args, swaps)],
+            out_specs=[spec(o.shape, False) for o in out_shapes],
+        ),
+        out_shape=out_shapes,
+        cost_estimate=pl.CostEstimate(flops=flops, bytes_accessed=moved, transcendentals=0),
+        compiler_params=pltpu.CompilerParams(vmem_limit_bytes=40 << 20),
+    )(partner, *args)
+
+
+def rounds_in_kernels(weights, factors, x1, e1, x2, own_in, own_out, partners, scales):
+    nrep, units, dim = weights[0].shape
+    nten = lax.axis_size("tensor")
+    rows = x1.shape[1]
+    like = jax.ShapeDtypeStruct((nrep, units, dim), BF16)
+    flops = 18 * nrep * units * rows * dim
+    res = over_replicas(
+        update_kernel,
+        scales,
+        partners[0],
+        list(weights) + [factors, x1, e1],
+        [x2],
+        [like] * 6
+        + [
+            jax.ShapeDtypeStruct((nrep, 2, units, rows), F32),
+            jax.ShapeDtypeStruct((nrep, units, rows), BF16),
+            jax.ShapeDtypeStruct((nrep, rows, dim), BF16),
+        ],
+        flops,
+    )
+    pre, hid, terms = res[6:]
+    e2 = exchange(terms, own_in, own_out, nrep, nten)
+    return over_replicas(
+        last_kernel, scales, partners[1], list(res[:6]) + [x2, e2, pre, hid], [], [like] * 3, flops
+    )
+
+
 def slice_step(weights, inputs, own_in, own_out, in_scale, hid_scale):
     w_gate, w_up, w_down = weights
     replicas, rows, dim = inputs.shape
@@ -180,16 +292,11 @@
     active = gate_pre * sigmoid_gate
     hidden = (active * up_value).astype(BF16)
     terms = (bdot(hidden, w_down, 2, 1) * hid_scale).astype(BF16)
-    nrep, nten = lax.axis_size("replica"), lax.axis_size("tensor")
-    total = nrep * nten
-    if total & (total - 1) == 0 and total * own_in.size <= 1 << 22:
-        errors = exchange(terms, own_in, own_out, nrep, nten)
-    else:
-        branch = lax.psum_scatter(
-            terms.reshape(replicas * rows, dim), AXES, scatter_dimension=0, tiled=True
-        ).astype(F32)
-        own_err = (own_in.astype(F32) + branch - own_out.astype(F32)).astype(BF16)
-        errors = lax.all_gather(own_err, AXES, axis=0, tiled=True).reshape(replicas, rows, dim)
+    branch = lax.psum_scatter(
+        terms.reshape(replicas * rows, dim), AXES, scatter_dimension=0, tiled=True
+    ).astype(F32)
+    own_err = (own_in.astype(F32) + branch - own_out.astype(F32)).astype(BF16)
+    errors = lax.all_gather(own_err, AXES, axis=0, tiled=True).reshape(replicas, rows, dim)
     back_grad = bdot(errors, w_down, 2, 2) * hid_scale
     delta_gate = (
         back_grad * up_value * sigmoid_gate * (1.0 + gate_pre * (1.0 - sigmoid_gate))
@@ -246,22 +353,31 @@
     full = full.transpose(1, 0, 2, 3).reshape(ROUNDS, nrep, rows, dim)
     all_errors = lax.all_gather(mine(errors, 0), AXES, axis=0, tiled=True).reshape(nrep, rows, dim)
     stacked = jnp.stack([f.reshape(nrep, units, rows) for f in factors], axis=1)
+    weights, stacked = lax.optimization_barrier((weights, stacked))
     factors = lax.all_to_all(stacked, "replica", 0, 0, tiled=True)
-
-    sides = (full[0], full[0], all_errors)
-    scales = (in_scale, in_scale, hid_scale)
-    moments = []
-    updated = []
-    for i in range(3):
-        grad = bdot(factors[:, i], sides[i], 2, 1) * scales[i]
-        stepped = (weights[i].astype(F32) - inner_rate * grad).astype(BF16)
-        pair = first_update(weights[i], stepped, partners[0])
-        updated.append(pair[0])
-        moments.append(pair[1])
-    stepped = slice_step(
-        tuple(updated), full[1], mine(inputs[1], 0), mine(targets[1], 0), in_scale, hid_scale
-    )
-    weights = tuple(last_update(w, s, m, partners[1]) for w, s, m in zip(updated, stepped, moments))
+    own_in, own_out = mine(inputs[1], 0), mine(targets[1], 0)
+
+    total = nrep * nten
+    if units % 16 == 0 and total & (total - 1) == 0 and total * own_in.size <= 1 << 22:
+        weights = rounds_in_kernels(
+            weights, factors, full[0], all_errors, full[1], own_in, own_out, partners,
+            (in_scale, hid_scale),
+        )
+    else:
+        sides = (full[0], full[0], all_errors)
+        scales = (in_scale, in_scale, hid_scale)
+        moments = []
+        updated = []
+        for i in range(3):
+            grad = bdot(factors[:, i], sides[i], 2, 1) * scales[i]
+            stepped = (weights[i].astype(F32) - inner_rate * grad).astype(BF16)
+            pair = first_update(weights[i], stepped, partners[0])
+            updated.append(pair[0])
+            moments.append(pair[1])
+        stepped = slice_step(tuple(updated), full[1], own_in, own_out, in_scale, hid_scale)
+        weights = tuple(
+            last_update(w, s, m, partners[1]) for w, s, m in zip(updated, stepped, moments)
+        )
 
     def home(w):
         return lax.all_to_all(w, "replica", 0, 0, tiled=True).reshape(units_home, dim)

time: 794 us -> 732 us (0.922)
  matrix products: 73.3 us -> 12.4 us
  Pallas kernels: 72.4 us -> 130 us
  other arithmetic: 33.5 us -> 4.56 us
  waiting for transfers between devices: 357 us -> 342 us
  local copies, waits for them, and re-layouts: 64.8 us -> 50.8 us
    dot_general x10 -> x0, matrix products: 61.5 us -> none  [bdot(): lax.dot_general(a, b, (((ca,), (cb,)), ((0,), (0,))), preferred_element_t...]
    pallas_call x0 -> x2, Pallas kernels: none -> 56.8 us  [over_replicas(): pl.pallas_call(functools.partial(kernel, scales), grid_spec=pltpu.Prefetc...]
    convert_element_type x2 -> x0, other arithmetic: 31.2 us -> none  [the longest x1 17.7 us: last_update(): return (0.05 * weight.astype(F32) + own + other).astype(BF16)]
    gather x6 -> x0, local copies, waits for them, and re-layouts: 25.7 us -> none  [the longest x3 12.8 us: first_update(): other = jnp.take(stepped, partner, axis=0)]
    psum x1, waiting for transfers between devices: 23.1 us -> 0.02 us  [home_step(): branch = lax.psum(term.astype(BF16), 'tensor').astype(F32)]
    all_to_all x3, waiting for transfers between devices: 220 us -> 238 us  [spread(): lax.all_to_all(w.reshape(nrep, units, dim), 'replica', 0, 0, tiled=True)]
    all_to_all x1, waiting for transfers between devices: 30.4 us -> 19.1 us  [body(): factors = lax.all_to_all(stacked, 'replica', 0, 0, tiled=True)]
    unnamed x33 -> x27, local copies, waits for them, and re-layouts: 6.63 us -> 15 us
  transfers between devices with their start and end apart: 9 -> 9, of which waited for: 7 -> 6; matrix products, arithmetic and copies ran while one was open for 7% -> 6% of each run, Pallas kernels for 0% -> 0%
where the time goes in v3:
time: 732 us; the launch traced here: 730 us
  waiting for transfers between devices  342 us (47%)
  blocking collectives  151 us (21%)
  Pallas kernels  130 us (18%)
  local copies, waits for them, and re-layouts  50.8 us (7%)
  starting transfers between devices  26 us (4%)
  between operations  13.9 us (2%)
  matrix products  12.4 us (2%)
    all_to_all x3, waiting for transfers between devices, spread(): lax.all_to_all(w.reshape(nrep, units, dim), 'replica', 0, 0, tiled=True)  238 us
    all_to_all x2, blocking collectives, home(): lax.all_to_all(w, 'replica', 0, 0, tiled=True).reshape(units_home, dim)  151 us
    pallas_call x1, Pallas kernels, exchange(): pl.pallas_call(functools.partial(exchange_kernel, plans, nrep, nten), out...  72.8 us
    all_to_all x1, waiting for transfers between devices, home(): lax.all_to_all(w, 'replica', 0, 0, tiled=True).reshape(units_home, dim)  62.4 us
    pallas_call x2, Pallas kernels, over_replicas(): pl.pallas_call(functools.partial(kernel, scales), grid_spec=pltpu.Prefetc...  56.8 us
    all_gather x1, waiting for transfers between devices, body(): lax.all_gather(jnp.stack([in_cols, out_cols]), 'tensor', axis=3, tiled=True)  22.4 us
    all_to_all x1, waiting for transfers between devices, body(): factors = lax.all_to_all(stacked, 'replica', 0, 0, tiled=True)  19.1 us
    all_to_all x3, starting transfers between devices, spread(): lax.all_to_all(w.reshape(nrep, units, dim), 'replica', 0, 0, tiled=True)  16.1 us
  transfers between devices with their start and end apart: 9, of which 6 were waited for; matrix products, arithmetic and copies ran while one was open for 6% of the time, Pallas kernels for 0%

profile of v3, /device:TPU:11, one launch (start us, length us, event | category | flops | bytes accessed | tf_op | source)
XLA Modules:
  0.0 729.7 jit_solution(10120455460389894495)
XLA Ops:
  11.7 22.4 %all-gather.4.cloned.1.call-done = bf16[2,2,128,1024]{3,2,1,0:T(8,128)(2,1)} async-done(((bf16[2,2,128,512]{3,2,1,0:T(8,128)(2,1)}), bf16[2,2,128,1024]{3,2,1,0:T(8,128)(2,1)}) %all-gather.4.cloned.1.call-update) | async-done | bytes 1048592 | tf_op jit(solution)/shard_map/all_gather | solution.py:349
  34.0 2.6 fusion.23
  36.7 3.9 multiply_convert_fusion.2
  43.8 6.5 all-to-all-start.2
  50.3 4.6 copy.17
  54.9 82.1 %all-to-all-done.2.refs_2_.refs_8_ = bf16[16,96,1024]{2,1,0:T(8,128)(2,1)S(1)} async-done(((bf16[16,96,1024]{2,1,0:T(8,128)(2,1)}), bf16[16,96,1024]{2,1,0:T(8,128)(2,1)S(1)}, u32[]{:S(2)}, u32[]{:S(2)}) %all-to-all-start.2) | async-done | bytes 3145760 | tf_op jit(solution)/shard_map/all_to_all | solution.py:335
  137.0 1.7 copy-done.6
  138.7 4.7 all-to-all-start.1
  146.1 4.6 copy.16
  150.8 82.4 %all-to-all-done.1.refs_1_.refs_7_ = bf16[16,96,1024]{2,1,0:T(8,128)(2,1)} async-done(((bf16[16,96,1024]{2,1,0:T(8,128)(2,1)}), bf16[16,96,1024]{2,1,0:T(8,128)(2,1)}, u32[]{:S(2)}, u32[]{:S(2)}) %all-to-all-start.1) | async-done | bytes 3145760 | tf_op jit(solution)/shard_map/all_to_all | solution.py:335
  233.1 4.9 all-to-all-start
  238.9 4.7 multiply_convert_fusion.1
  243.6 1.9 copy.18
  245.5 1.9 copy.19
  247.4 2.2 pad_maximum_fusion
  249.7 73.1 %all-to-all-done.refs_0_.refs_6_ = bf16[16,96,1024]{2,1,0:T(8,128)(2,1)S(1)} async-done(((bf16[16,96,1024]{2,1,0:T(8,128)(2,1)}), bf16[16,96,1024]{2,1,0:T(8,128)(2,1)S(1)}, u32[]{:S(2)}, u32[]{:S(2)}) %all-to-all-start) | async-done | bytes 3145760 | tf_op jit(solution)/shard_map/all_to_all | solution.py:335
  322.8 1.7 copy-done.7
  324.5 4.6 all-to-all-start.3
  331.5 6.2 fusion.36
  337.8 19.1 %all-to-all-done.3.refs_3_.refs_9_ = bf16[16,3,96,128]{3,2,1,0:T(8,128)(2,1)S(1)} async-done(((bf16[16,3,96,128]{3,2,1,0:T(8,128)(2,1)}), bf16[16,3,96,128]{3,2,1,0:T(8,128)(2,1)S(1)}, u32[]{:S(2)}, u32[]{:S(2)}) %all-to-all-start.3) | async-done | bytes 1179680 | tf_op jit(solution)/shard_map/all_to_all | solution.py:357
  356.9 27.6 %shard_map.85 = (bf16[16,96,1024]{2,1,0:T(8,128)(2,1)S(1)}, bf16[16,96,1024]{2,1,0:T(8,128)(2,1)S(1)}, bf16[16,96,1024]{2,1,0:T(8,128)(2,1)S(1)}, bf16[16,96,102...) custom-call(s32[16]{0:T(128)S(1)} %get-tuple-element.44.partner, ...), custom_call_target="tpu_custom_call" | custom-call | flops 3623878656 | bytes 42205184 | tf_op jit(solution)/shard_map/pallas_call | solution.py:245
  386.2 1.7 copy-done.4
  389.5 72.8 %shard_map.86 = bf16[2,2,2,2,2,64,1024]{6,5,4,3,2,1,0:T(8,128)(2,1)} custom-call(bf16[2,2,2,2,2,64,1024]{6,5,4,3,2,1,0:T(8,128)(2,1)} %bitcast.117, bf16[64,1024]{1,0:T(8,128)(2,1)} %dynamic-slice_bitcast_fusion.1.own_in, bf16[64,1024]{1,0:T(8,128)(2,1)} %dynamic-slice_bitcast_fusion.own_out), custom_call_target="tpu_custom_call" | custom-call | tf_op jit(solution)/shard_map/pallas_call | solution.py:161
  462.3 1.9 copy-done.3
  464.2 29.2 %shard_map.87 = (bf16[16,96,1024]{2,1,0:T(8,128)(2,1)S(1)}, bf16[16,96,1024]{2,1,0:T(8,128)(2,1)S(1)}, bf16[16,96,1024]{2,1,0:T(8,128)(2,1)}) custom-call(s32[16]{0:T(128)S(1)} %get-tuple-element.45.partner, bf16[16,96,1024]{2,1,0:T(8,128)(2,1)S(1)} %copy-done.3, bf16[16,96,1024]{2,1,0:T(8,128)(2,1)} %copy-done.4, bf16[16,96,1024]{2,1,0:T(8,128)(2,1)} %copy-done.5, ...), custom_call_target="tpu_custom_call" | custom-call | flops 3623878656 | bytes 58458112 | tf_op jit(solution)/shard_map/pallas_call | solution.py:245
  493.4 76.0 %all_to_all.35 = bf16[16,96,1024]{2,1,0:T(8,128)(2,1)S(1)} all-to-all(bf16[16,96,1024]{2,1,0:T(8,128)(2,1)S(1)} %get-tuple-element.33), channel_id=1, replica_groups=mesh['replica'=16,'tensor'=2] {'replica'}, dimensions={0} | all-to-all | bytes 6291456 | tf_op jit(solution)/shard_map/all_to_all | solution.py:383
  569.4 74.7 %all_to_all.36 = bf16[16,96,1024]{2,1,0:T(8,128)(2,1)} all-to-all(bf16[16,96,1024]{2,1,0:T(8,128)(2,1)S(1)} %get-tuple-element.34), channel_id=1, replica_groups=mesh['replica'=16,'tensor'=2] {'replica'}, dimensions={0} | all-to-all | bytes 6291456 | tf_op jit(solution)/shard_map/all_to_all | solution.py:383
  644.1 5.1 all-to-all-start.6
  649.2 2.9 copy.21
  652.2 4.6 copy.22
  656.8 62.4 %all-to-all-done.6 = bf16[16,96,1024]{2,1,0:T(8,128)(2,1)} async-done(((bf16[16,96,1024]{2,1,0:T(8,128)(2,1)}), bf16[16,96,1024]{2,1,0:T(8,128)(2,1)}, u32[]{:S(2)}, u32[]{:S(2)}) %all-to-all-start.6) | async-done | bytes 3145760 | tf_op jit(solution)/shard_map/all_to_all | solution.py:383
  719.2 3.9 copy.25
  (53 shorter events, 16.9 us)
Async XLA Ops:
  7.2 1.1 copy-start
  7.2 26.9 %all-gather.4.cloned.1.call-start = ((), (), s32[]{:S(2)}) async-start(), calls=%async_computation.7 | async-start | bytes 1572864 | tf_op jit(solution)/shard_map/all_gather | solution.py:349
  11.6 131.8 %all-reduce.2.cloned.1.call-start = ((), (), s32[]{:S(2)}) async-start(), calls=%async_computation.8 | async-start | bytes 524288 | tf_op jit(solution)/shard_map/psum | solution.py:34
  36.6 3.9 copy-start.10
  36.6 3.9 copy-start.8
  41.9 289.6 %all-gather.6.cloned.1.call-start = ((), (), s32[]{:S(2)}) async-start(), calls=%async_computation.9 | async-start | bytes 8650752 | tf_op jit(solution)/shard_map/all_gather | solution.py:352
  43.8 93.2 %all-to-all-start.2 = ((bf16[16,96,1024]{2,1,0:T(8,128)(2,1)}), bf16[16,96,1024]{2,1,0:T(8,128)(2,1)S(1)}, u32[]{:S(2)}, u32[]{:S(2)}) async-start(bf16[16,96,1024]{2,1,0:T(8,128)(2,1)} %bitcast.115), calls=%async_computation.2 | async-start | bytes 6291456 | tf_op jit(solution)/shard_map/all_to_all | solution.py:335
  137.0 1.7 copy-start.6
  138.7 94.5 %all-to-all-start.1 = ((bf16[16,96,1024]{2,1,0:T(8,128)(2,1)}), bf16[16,96,1024]{2,1,0:T(8,128)(2,1)}, u32[]{:S(2)}, u32[]{:S(2)}) async-start(bf16[16,96,1024]{2,1,0:T(8,128)(2,1)} %bitcast.112), calls=%async_computation.1 | async-start | bytes 6291456 | tf_op jit(solution)/shard_map/all_to_all | solution.py:335
  143.4 213.5 %all-gather.8.cloned.1.call-start = ((), (), s32[]{:S(2)}) async-start(), calls=%async_computation.10 | async-start | bytes 4325376 | tf_op jit(solution)/shard_map/all_gather | solution.py:354
  144.7 0.7 copy-start.11
  233.1 89.7 %all-to-all-start = ((bf16[16,96,1024]{2,1,0:T(8,128)(2,1)}), bf16[16,96,1024]{2,1,0:T(8,128)(2,1)S(1)}, u32[]{:S(2)}, u32[]{:S(2)}) async-start(bf16[16,96,1024]{2,1,0:T(8,128)(2,1)} %bitcast.111), calls=%async_computation | async-start | bytes 6291456 | tf_op jit(solution)/shard_map/all_to_all | solution.py:335
  238.9 8.5 %copy-start.9 = (bf16[1536,128]{1,0:T(8,128)(2,1)S(1)}, bf16[1536,128]{1,0:T(8,128)(2,1)}, u32[]{:S(2)}) copy-start(bf16[1536,128]{1,0:T(8,128)(2,1)} %copy.20) | copy-start | bytes 1179652
  243.6 85.5 %copy-start.12 = (s32[2,16]{1,0:T(2,128)S(1)}, s32[2,16]{1,0:T(2,128)}, u32[]{:S(2)}) copy-start(s32[2,16]{1,0:T(2,128)} %param.13) | copy-start | bytes 388
  322.8 1.7 copy-start.7
  324.5 32.4 %all-to-all-start.3 = ((bf16[16,3,96,128]{3,2,1,0:T(8,128)(2,1)}), bf16[16,3,96,128]{3,2,1,0:T(8,128)(2,1)S(1)}, u32[]{:S(2)}, u32[]{:S(2)}) async-start(bf16[16,3,96,128]{3,2,1,0:T(8,128)(2,1)} %pad_maximum_fusion), calls=%async_computation.3 | async-start | bytes 2359296 | tf_op jit(solution)/shard_map/all_to_all | solution.py:357
  384.5 1.7 copy-start.2
  386.2 1.7 copy-start.4
  387.8 1.6 copy-start.5
  462.3 1.9 copy-start.3
  644.1 75.1 %all-to-all-start.6 = ((bf16[16,96,1024]{2,1,0:T(8,128)(2,1)}), bf16[16,96,1024]{2,1,0:T(8,128)(2,1)}, u32[]{:S(2)}, u32[]{:S(2)}) async-start(bf16[16,96,1024]{2,1,0:T(8,128)(2,1)} %get-tuple-element.35), calls=%async_computation.6 | async-start | bytes 6291456 | tf_op jit(solution)/shard_map/all_to_all | solution.py:383
  719.2 3.9 copy-start.1
Sparse Core Ops, SparseCore 0:
  11.8 22.2 all-gather.3
  42.0 23.1 all-reduce.1
  68.3 126.2 all-gather.5
  197.3 108.2 all-gather.7

commit v4 on v3

--- a/solution.py
+++ b/solution.py
@@ -149,14 +149,21 @@
     nbits = (nrep * nten).bit_length() - 1
     tbits = nten.bit_length() - 1
     ring = list(range(tbits)) + list(range(tbits + 1, nbits))
-    half = dim // 2
-    orders = ([tbits] + ring, [tbits] + ring[tbits:] + ring[:tbits])
-    plans = [((i * half, half), orders[i]) for i in range(2)]
+    near, far = ring[: tbits + 1], ring[tbits + 1 :]
+    turned = near[::-1]
+    orders = [
+        [tbits] + near + far,
+        [tbits] + turned + far,
+        [tbits] + turned[:1] + far + turned[1:],
+        [tbits] + near[:1] + far + near[1:],
+    ]
+    half = dim // len(orders)
+    plans = [((i * half, half), order) for i, order in enumerate(orders)]
     view = (2,) * nbits + (rows, dim)
     scratch = [
         pltpu.VMEM((2,) * (nbits - 1 - s) + (rows, half), BF16) for _ in plans for s in range(nbits)
     ]
-    scratch += [pltpu.SemaphoreType.DMA((2, 2 * nbits))] * 2
+    scratch += [pltpu.SemaphoreType.DMA((len(plans), 2 * nbits))] * 2
     vmem = pl.BlockSpec(memory_space=pltpu.VMEM)
     out = pl.pallas_call(
         functools.partial(exchange_kernel, plans, nrep, nten),
@@ -207,27 +214,38 @@
     terms[0] = term.astype(BF16)
 
 
-def last_kernel(scales, partner, *refs):
-    own, other, outs = refs[:10], refs[10:20], refs[20:]
+def share_of(weight, moment, fac, side, scale):
+    grad = jnp.dot(fac, side, preferred_element_type=F32) * scale
+    local = (weight.astype(F32) - inner_rate * grad).astype(BF16).astype(F32)
+    return 0.475 * local - 0.2025 * moment.astype(F32)
+
+
+def joined(weight, mine, theirs):
+    return (0.05 * weight.astype(F32) + mine + theirs.astype(BF16).astype(F32)).astype(BF16)
+
+
+def last_down_kernel(scales, partner, *refs):
+    own, other, out = refs[:4], refs[4:8], refs[8]
+    mine, theirs = (share_of(*(ref[0] for ref in group), scales[1]) for group in (own, other))
+    out[0] = joined(own[0][0], mine, theirs)
+
+
+def last_units_kernel(scales, partner, *refs):
+    own, other, outs = refs[:8], refs[8:16], refs[16:]
     in_scale, hid_scale = scales
 
     def shares(group):
-        x2, e2, pre, hid = group[6][0], group[7][0], group[8], group[9][0]
+        down, x2, e2, pre = group[4][0], group[5][0], group[6][0], group[7]
         gate_pre, up_value = pre[0, 0], pre[0, 1]
-        back = dot_in(group[2][0], e2) * hid_scale
+        back = dot_in(down, e2) * hid_scale
         sig = jax.nn.sigmoid(gate_pre)
         delta_gate = (back * up_value * sig * (1.0 + gate_pre * (1.0 - sig))).astype(BF16)
         delta_up = (back * (gate_pre * sig)).astype(BF16)
-        for i, (fac, side, scale) in enumerate(
-            ((delta_gate, x2, in_scale), (delta_up, x2, in_scale), (hid, e2, hid_scale))
-        ):
-            grad = jnp.dot(fac, side, preferred_element_type=F32) * scale
-            local = (group[i][0].astype(F32) - inner_rate * grad).astype(BF16).astype(F32)
-            yield 0.475 * local - 0.2025 * group[3 + i][0].astype(F32)
+        for i, fac in enumerate((delta_gate, delta_up)):
+            yield share_of(group[i][0], group[2 + i][0], fac, x2, in_scale)
 
     for i, (mine, theirs) in enumerate(zip(shares(own), shares(other))):
-        total = 0.05 * own[i][0].astype(F32) + mine + theirs.astype(BF16).astype(F32)
-        outs[i][0] = total.astype(BF16)
+        outs[i][0] = joined(own[i][0], mine, theirs)
 
 
 def over_replicas(kernel, scales, partner, paired, single, out_shapes, flops):
@@ -278,9 +296,16 @@
     )
     pre, hid, terms = res[6:]
     e2 = exchange(terms, own_in, own_out, nrep, nten)
-    return over_replicas(
-        last_kernel, scales, partners[1], list(res[:6]) + [x2, e2, pre, hid], [], [like] * 3, flops
+    gate, up, down = res[:3]
+    down_new = over_replicas(
+        last_down_kernel, scales, partners[1], [down, res[5], hid, e2], [], [like], flops // 3
+    )[0]
+    down_new, row = lax.optimization_barrier((down_new, partners[1]))
+    gate_new, up_new = over_replicas(
+        last_units_kernel, scales, row, [gate, up, res[3], res[4], down, x2, e2, pre], [],
+        [like] * 2, flops,
     )
+    return gate_new, up_new, down_new
 
 
 def slice_step(weights, inputs, own_in, own_out, in_scale, hid_scale):
@@ -382,7 +407,8 @@
     def home(w):
         return lax.all_to_all(w, "replica", 0, 0, tiled=True).reshape(units_home, dim)
 
-    return (home(weights[0]).T[None], home(weights[1]).T[None], home(weights[2])[None])
+    down_home, gate, up = lax.optimization_barrier((home(weights[2]), weights[0], weights[1]))
+    return (home(gate).T[None], home(up).T[None], down_home[None])
 
 
 def solution(mesh):

time: 732 us -> 714 us (0.975)
  blocking collectives: 151 us -> 75.3 us
  waiting for transfers between devices: 342 us -> 384 us
  local copies, waits for them, and re-layouts: 50.8 us -> 62.6 us
    all_to_all x2 -> x1, blocking collectives: 151 us -> 75.3 us  [home(): lax.all_to_all(w, 'replica', 0, 0, tiled=True).reshape(units_home, dim)]
    all_to_all x1 -> x2, waiting for transfers between devices: 62.4 us -> 105 us  [home(): lax.all_to_all(w, 'replica', 0, 0, tiled=True).reshape(units_home, dim)]
    unnamed x27 -> x43, local copies, waits for them, and re-layouts: 15 us -> 26.8 us
    pallas_call x2 -> x3, Pallas kernels: 56.8 us -> 61.1 us  [over_replicas(): pl.pallas_call(functools.partial(kernel, scales), grid_spec=pltpu.Prefetc...]
  transfers between devices with their start and end apart: 9 -> 10, of which waited for: 6 -> 7; matrix products, arithmetic and copies ran while one was open for 6% -> 5% of each run, Pallas kernels for 0% -> 3%
where the time goes in v4:
time: 714 us; the launch traced here: 712 us
  waiting for transfers between devices  384 us (54%)
  Pallas kernels  127 us (18%)
  blocking collectives  75.3 us (11%)
  local copies, waits for them, and re-layouts  62.6 us (9%)
  starting transfers between devices  32.1 us (4%)
  between operations  14 us (2%)
  matrix products  12.4 us (2%)
    all_to_all x3, waiting for transfers between devices, spread(): lax.all_to_all(w.reshape(nrep, units, dim), 'replica', 0, 0, tiled=True)  238 us
    all_to_all x2, waiting for transfers between devices, home(): lax.all_to_all(w, 'replica', 0, 0, tiled=True).reshape(units_home, dim)  105 us
    all_to_all x1, blocking collectives, home(): lax.all_to_all(w, 'replica', 0, 0, tiled=True).reshape(units_home, dim)  75.3 us
    pallas_call x1, Pallas kernels, exchange(): pl.pallas_call(functools.partial(exchange_kernel, plans, nrep, nten), out...  66 us
    pallas_call x3, Pallas kernels, over_replicas(): pl.pallas_call(functools.partial(kernel, scales), grid_spec=pltpu.Prefetc...  61.1 us
    unnamed x43, local copies, waits for them, and re-layouts  26.8 us
    all_gather x1, waiting for transfers between devices, body(): lax.all_gather(jnp.stack([in_cols, out_cols]), 'tensor', axis=3, tiled=True)  22.4 us
    all_to_all x1, waiting for transfers between devices, body(): factors = lax.all_to_all(stacked, 'replica', 0, 0, tiled=True)  19.1 us
  transfers between devices with their start and end apart: 10, of which 7 were waited for; matrix products, arithmetic and copies ran while one was open for 5% of the time, Pallas kernels for 3%

profile of v4, /device:TPU:11, one launch (start us, length us, event | category | flops | bytes accessed | tf_op | source)
XLA Modules:
  0.0 712.2 jit_solution(7629523862630536958)
XLA Ops:
  11.7 22.4 %all-gather.4.cloned.1.call-done = bf16[2,2,128,1024]{3,2,1,0:T(8,128)(2,1)} async-done(((bf16[2,2,128,512]{3,2,1,0:T(8,128)(2,1)}), bf16[2,2,128,1024]{3,2,1,0:T(8,128)(2,1)}) %all-gather.4.cloned.1.call-update) | async-done | bytes 1048592 | tf_op jit(solution)/shard_map/all_gather | solution.py:374
  34.0 2.6 fusion.23
  36.6 3.9 multiply_convert_fusion.2
  43.7 6.5 all-to-all-start.2
  50.3 4.6 copy.17
  54.9 82.1 %all-to-all-done.2.refs_2_.refs_8_ = bf16[16,96,1024]{2,1,0:T(8,128)(2,1)S(1)} async-done(((bf16[16,96,1024]{2,1,0:T(8,128)(2,1)}), bf16[16,96,1024]{2,1,0:T(8,128)(2,1)S(1)}, u32[]{:S(2)}, u32[]{:S(2)}) %all-to-all-start.2) | async-done | bytes 3145760 | tf_op jit(solution)/shard_map/all_to_all | solution.py:360
  138.6 4.7 all-to-all-start.1
  146.1 4.6 copy.16
  150.7 82.4 %all-to-all-done.1.refs_1_.refs_7_ = bf16[16,96,1024]{2,1,0:T(8,128)(2,1)} async-done(((bf16[16,96,1024]{2,1,0:T(8,128)(2,1)}), bf16[16,96,1024]{2,1,0:T(8,128)(2,1)}, u32[]{:S(2)}, u32[]{:S(2)}) %all-to-all-start.1) | async-done | bytes 3145760 | tf_op jit(solution)/shard_map/all_to_all | solution.py:360
  233.1 4.9 all-to-all-start
  238.9 4.6 multiply_convert_fusion.1
  243.5 1.9 copy.18
  245.5 1.9 copy.19
  247.4 2.2 pad_maximum_fusion
  249.7 73.2 %all-to-all-done.refs_0_.refs_6_ = bf16[16,96,1024]{2,1,0:T(8,128)(2,1)S(1)} async-done(((bf16[16,96,1024]{2,1,0:T(8,128)(2,1)}), bf16[16,96,1024]{2,1,0:T(8,128)(2,1)S(1)}, u32[]{:S(2)}, u32[]{:S(2)}) %all-to-all-start) | async-done | bytes 3145760 | tf_op jit(solution)/shard_map/all_to_all | solution.py:360
  324.5 4.6 all-to-all-start.3
  331.5 6.2 fusion.36
  337.7 19.1 %all-to-all-done.3.refs_3_.refs_9_ = bf16[16,3,96,128]{3,2,1,0:T(8,128)(2,1)S(1)} async-done(((bf16[16,3,96,128]{3,2,1,0:T(8,128)(2,1)}), bf16[16,3,96,128]{3,2,1,0:T(8,128)(2,1)S(1)}, u32[]{:S(2)}, u32[]{:S(2)}) %all-to-all-start.3) | async-done | bytes 1179680 | tf_op jit(solution)/shard_map/all_to_all | solution.py:382
  356.8 27.6 %shard_map.85 = (bf16[16,96,1024]{2,1,0:T(8,128)(2,1)S(1)}, bf16[16,96,1024]{2,1,0:T(8,128)(2,1)S(1)}, bf16[16,96,1024]{2,1,0:T(8,128)(2,1)S(1)}, bf16[16,96,102...) custom-call(s32[16]{0:T(128)S(1)} %get-tuple-element.52.partner, ...), custom_call_target="tpu_custom_call" | custom-call | flops 3623878656 | bytes 42205184 | tf_op jit(solution)/shard_map/pallas_call | solution.py:263
  390.6 66.0 %shard_map.86 = bf16[2,2,2,2,2,64,1024]{6,5,4,3,2,1,0:T(8,128)(2,1)} custom-call(bf16[2,2,2,2,2,64,1024]{6,5,4,3,2,1,0:T(8,128)(2,1)} %bitcast.120, bf16[64,1024]{1,0:T(8,128)(2,1)} %dynamic-slice_bitcast_fusion.1.own_in, bf16[64,1024]{1,0:T(8,128)(2,1)} %dynamic-slice_bitcast_fusion.own_out), custom_call_target="tpu_custom_call" | custom-call | tf_op jit(solution)/shard_map/pallas_call | solution.py:168
  456.6 2.2 copy-done.2
  458.8 1.9 copy-done.4
  462.6 9.9 %shard_map.87 = bf16[16,96,1024]{2,1,0:T(8,128)(2,1)} custom-call(s32[16]{0:T(128)S(1)} %get-tuple-element.33.partner, bf16[16,96,1024]{2,1,0:T(8,128)(2,1)S(1)} %copy-done.4, bf16[16,96,1024]{2,1,0:T(8,128)(2,1)S(1)} %copy-done.5, bf16[16,96,128]{2,1,0:T(8,128)(2,1)S(1)} %get-tuple-element.30.refs_2_.refs_6_, bf16[16,128,1024]{2,1,0:T(8,128)(2,1)S(1)} %bitcast.104, ...), custom_call_target="tpu_custom_call" | custom-call | flops 1207959552 | bytes 21757952 | tf_op jit(solution)/shard_map/pallas_call | solution.py:263
  472.4 6.1 all-to-all-start.4
  481.8 23.6 %shard_map.88 = (bf16[16,96,1024]{2,1,0:T(8,128)(2,1)S(1)}, bf16[16,96,1024]{2,1,0:T(8,128)(2,1)S(1)}) custom-call(s32[16]{0:T(128)S(1)} %get-tuple-element.33.partner, bf16[16,96,1024]{2,1,0:T(8,128)(2,1)S(1)} %copy-done.7, bf16[16,96,1024]{2,1,0:T(8,128)(2,1)S(1)} %copy-done.9, bf16[16,96,1024]{2,1,0:T(8,128)(2,1)} %get-tuple-element.36.refs_2_.refs_10_, ...), custom_call_target="tpu_custom_call" | custom-call | flops 3623878656 | bytes 51380224 | tf_op jit(solution)/shard_map/pallas_call | solution.py:263
  508.8 39.8 %all-to-all-done.4 = bf16[16,96,1024]{2,1,0:T(8,128)(2,1)} async-done(((bf16[16,96,1024]{2,1,0:T(8,128)(2,1)}), bf16[16,96,1024]{2,1,0:T(8,128)(2,1)}, u32[]{:S(2)}, u32[]{:S(2)}) %all-to-all-start.4) | async-done | bytes 3145760 | tf_op jit(solution)/shard_map/all_to_all | solution.py:408
  548.5 75.3 %all_to_all.35 = bf16[16,96,1024]{2,1,0:T(8,128)(2,1)} all-to-all(bf16[16,96,1024]{2,1,0:T(8,128)(2,1)} %copy-done.13), channel_id=1, replica_groups=mesh['replica'=16,'tensor'=2] {'replica'}, dimensions={0} | all-to-all | bytes 6291456 | tf_op jit(solution)/shard_map/all_to_all | solution.py:408
  623.8 5.1 all-to-all-start.6
  628.9 4.6 copy.21
  633.6 65.3 %all-to-all-done.6 = bf16[16,96,1024]{2,1,0:T(8,128)(2,1)S(1)} async-done(((bf16[16,96,1024]{2,1,0:T(8,128)(2,1)}), bf16[16,96,1024]{2,1,0:T(8,128)(2,1)S(1)}, u32[]{:S(2)}, u32[]{:S(2)}) %all-to-all-start.6) | async-done | bytes 3145760 | tf_op jit(solution)/shard_map/all_to_all | solution.py:408
  698.8 2.9 copy.22
  701.7 3.9 copy.25
  (71 shorter events, 31.6 us)
Async XLA Ops:
  7.2 1.1 copy-start
  7.2 26.9 %all-gather.4.cloned.1.call-start = ((), (), s32[]{:S(2)}) async-start(), calls=%async_computation.7 | async-start | bytes 1572864 | tf_op jit(solution)/shard_map/all_gather | solution.py:374
  11.6 131.8 %all-reduce.2.cloned.1.call-start = ((), (), s32[]{:S(2)}) async-start(), calls=%async_computation.8 | async-start | bytes 524288 | tf_op jit(solution)/shard_map/psum | solution.py:34
  36.6 3.9 copy-start.18
  36.6 3.9 copy-start.16
  41.9 289.7 %all-gather.6.cloned.1.call-start = ((), (), s32[]{:S(2)}) async-start(), calls=%async_computation.9 | async-start | bytes 8650752 | tf_op jit(solution)/shard_map/all_gather | solution.py:377
  43.7 93.2 %all-to-all-start.2 = ((bf16[16,96,1024]{2,1,0:T(8,128)(2,1)}), bf16[16,96,1024]{2,1,0:T(8,128)(2,1)S(1)}, u32[]{:S(2)}, u32[]{:S(2)}) async-start(bf16[16,96,1024]{2,1,0:T(8,128)(2,1)} %bitcast.118), calls=%async_computation.2 | async-start | bytes 6291456 | tf_op jit(solution)/shard_map/all_to_all | solution.py:360
  137.0 1.7 copy-start.14
  138.6 94.5 %all-to-all-start.1 = ((bf16[16,96,1024]{2,1,0:T(8,128)(2,1)}), bf16[16,96,1024]{2,1,0:T(8,128)(2,1)}, u32[]{:S(2)}, u32[]{:S(2)}) async-start(bf16[16,96,1024]{2,1,0:T(8,128)(2,1)} %bitcast.115), calls=%async_computation.1 | async-start | bytes 6291456 | tf_op jit(solution)/shard_map/all_to_all | solution.py:360
  143.4 213.5 %all-gather.8.cloned.1.call-start = ((), (), s32[]{:S(2)}) async-start(), calls=%async_computation.10 | async-start | bytes 4325376 | tf_op jit(solution)/shard_map/all_gather | solution.py:379
  144.7 0.7 copy-start.19
  233.1 89.7 %all-to-all-start = ((bf16[16,96,1024]{2,1,0:T(8,128)(2,1)}), bf16[16,96,1024]{2,1,0:T(8,128)(2,1)S(1)}, u32[]{:S(2)}, u32[]{:S(2)}) async-start(bf16[16,96,1024]{2,1,0:T(8,128)(2,1)} %bitcast.114), calls=%async_computation | async-start | bytes 6291456 | tf_op jit(solution)/shard_map/all_to_all | solution.py:360
  238.9 8.5 %copy-start.17 = (bf16[1536,128]{1,0:T(8,128)(2,1)S(1)}, bf16[1536,128]{1,0:T(8,128)(2,1)}, u32[]{:S(2)}) copy-start(bf16[1536,128]{1,0:T(8,128)(2,1)} %copy.20) | copy-start | bytes 1179652
  243.5 85.5 %copy-start.20 = (s32[2,16]{1,0:T(2,128)S(1)}, s32[2,16]{1,0:T(2,128)}, u32[]{:S(2)}) copy-start(s32[2,16]{1,0:T(2,128)} %param.13) | copy-start | bytes 388
  322.8 1.7 copy-start.15
  324.5 32.4 %all-to-all-start.3 = ((bf16[16,3,96,128]{3,2,1,0:T(8,128)(2,1)}), bf16[16,3,96,128]{3,2,1,0:T(8,128)(2,1)S(1)}, u32[]{:S(2)}, u32[]{:S(2)}) async-start(bf16[16,3,96,128]{3,2,1,0:T(8,128)(2,1)} %pad_maximum_fusion), calls=%async_computation.3 | async-start | bytes 2359296 | tf_op jit(solution)/shard_map/all_to_all | solution.py:382
  384.5 1.6 copy-start.3
  386.1 1.7 copy-start.6
  387.8 1.7 copy-start.8
  389.4 1.2 copy-start.10
  456.6 2.2 copy-start.2
  458.8 1.9 copy-start.4
  460.7 1.9 copy-start.5
  472.4 6.1 copy-start.7
  472.4 76.1 %all-to-all-start.4 = ((bf16[16,96,1024]{2,1,0:T(8,128)(2,1)}), bf16[16,96,1024]{2,1,0:T(8,128)(2,1)}, u32[]{:S(2)}, u32[]{:S(2)}) async-start(bf16[16,96,1024]{2,1,0:T(8,128)(2,1)} %shard_map.87), calls=%async_computation.4 | async-start | bytes 6291456 | tf_op jit(solution)/shard_map/all_to_all | solution.py:408
  478.5 1.9 copy-start.9
  480.4 1.4 copy-start.11
  505.4 1.7 copy-start.12
  507.1 1.7 copy-start.13
  623.8 75.0 %all-to-all-start.6 = ((bf16[16,96,1024]{2,1,0:T(8,128)(2,1)}), bf16[16,96,1024]{2,1,0:T(8,128)(2,1)S(1)}, u32[]{:S(2)}, u32[]{:S(2)}) async-start(bf16[16,96,1024]{2,1,0:T(8,128)(2,1)} %copy-done.12), calls=%async_computation.6 | async-start | bytes 6291456 | tf_op jit(solution)/shard_map/all_to_all | solution.py:408
  701.7 3.9 copy-start.1
Sparse Core Ops, SparseCore 0:
  11.8 22.2 all-gather.3
  42.0 23.1 all-reduce.1
  68.2 126.2 all-gather.5
  197.3 108.2 all-gather.7
